TPU v7x, 256 devices: a whole 4x4x8 slice. The times are simulated.
256 devices in a mesh: chan: 4 (over x), vox: 64 (over y, z, core).
Axes of the slice: x: 4, y: 4, z: 8, core: 2. Of those that a mesh axis runs over, the one named last changes fastest.
Arguments:
- echo_data: bfloat16 [1024, 64, 6400], P('chan', 'vox'), may hold values from -60 to 60
- delays: int32 [1024, 64], P('chan', 'vox'), may hold values from 0 to 64, as said below
- aperture: int32 [128, 64], replicated, may hold values from 0 to 1, as said below
- offset: float32 [128, 64], P(None, 'vox'), may hold values from 0.5 to 3.2
- depth_slope: float32 [128, 64], P(None, 'vox'), may hold values from 0.3 to 0.4
- lateral_tilt: float32 [128, 64], P(None, 'vox'), may hold values from 0.075 to 0.125
- prior_basis: float32 [100, 30], replicated, may hold values from -6 to 6
Outputs:
- power: float32 [64, 16384], P('vox', 'chan')
Inputs may be any that keep to these rules, and one draw needn't show every extreme that they name: `delays`: every slab has a channel whose delay is 64. `aperture`: for each slab, the active blocks among the 32 blocks of one channel group (blocks g * 32 onward) form one cyclic run of at least 4 and at most 16 blocks; each channel group has exactly 16 active blocks in some slab.
All inputs are finite; a program needn't handle non-finite values.
Results may differ from a plain program's by a relative error of at most 0.0075.
Values may be sent and summed in bfloat16 or wider, within the bound.
A program may use at most 128 MiB of HBM per device.

v0:
```python
import math

import jax
import jax.numpy as jnp
from jax import lax
from jax.sharding import PartitionSpec as P

CHANNELS = 1024
FRAMES = 100
BLOCK_CH = 8
WINDOW = 64
DEPTH_VOX = 64
SLAB_VOX = 16384


def passed_along(block, axis, distance):
    devices = range(lax.axis_size(axis))
    route = [(i - distance, i) for i in devices if i - distance in devices]
    return lax.ppermute(block, axis, route)


def interp_table(offsets, slopes, tilts, first_voxel, voxel_count):
    voxel = first_voxel + jnp.arange(voxel_count)
    lateral = (voxel // DEPTH_VOX).astype(jnp.float32)
    depth = (voxel % DEPTH_VOX).astype(jnp.float32)
    position = (
        offsets[:, None] + slopes[:, None] * depth[None, :] + tilts[:, None] * lateral[None, :]
    )
    sample_rows = jnp.arange(WINDOW).astype(jnp.float32)
    weights = jnp.maximum(0.0, 1.0 - jnp.abs(sample_rows[None, :, None] - position[:, None, :]))
    return (weights / math.sqrt(CHANNELS)).astype(jnp.bfloat16)


def take_window(row, start):
    return lax.dynamic_slice(row, (jnp.zeros((), jnp.int32), start), (row.shape[0], WINDOW))


def refine_basis(gram_matrix, prior_basis):
    basis = prior_basis
    for sweep in range(2):
        product = jnp.dot(gram_matrix, basis, precision=lax.Precision.HIGHEST)
        normal_matrix = jnp.dot(product.T, product, precision=lax.Precision.HIGHEST)
        factor = jnp.linalg.cholesky(normal_matrix)
        basis = jax.scipy.linalg.solve_triangular(factor, product.T, lower=True).T
    return basis


def project(summed, geometry, first_voxel, voxel_count):
    block_count, frames = (summed.shape[0], summed.shape[1])
    width = math.gcd(block_count, 4)
    turns = block_count // width
    inputs = (
        summed.reshape(turns, width, frames, WINDOW),
        geometry[0].reshape(turns, width),
        geometry[1].reshape(turns, width),
        geometry[2].reshape(turns, width),
    )

    def one_turn(accumulated, pieces):
        table = interp_table(pieces[1], pieces[2], pieces[3], first_voxel, voxel_count)
        added = jnp.einsum("bfk,bkv->fv", pieces[0], table, preferred_element_type=jnp.float32)
        return (accumulated + added, None)

    start = jnp.zeros((frames, voxel_count), jnp.float32)
    result, unused = lax.scan(one_turn, start, inputs)
    return result


def body(echo_data, delays, aperture, offset, depth_slope, lateral_tilt, prior_basis):
    block_count = echo_data.shape[0] // BLOCK_CH
    frames = FRAMES
    slab = lax.axis_index("vox")
    group = lax.axis_index("chan")
    group_count = lax.axis_size("chan")
    gate_table = lax.dynamic_index_in_dim(aperture, slab, 1, keepdims=False).reshape(
        group_count, block_count
    )
    offset_table = offset[:, 0].reshape(group_count, block_count)
    slope_table = depth_slope[:, 0].reshape(group_count, block_count)
    tilt_table = lateral_tilt[:, 0].reshape(group_count, block_count)
    own_gates = lax.dynamic_index_in_dim(gate_table, group, 0, keepdims=False)
    echo_rows = echo_data.reshape(block_count, BLOCK_CH, frames * WINDOW)
    block_delays = delays[:, 0].reshape(block_count, BLOCK_CH)
    upper_rows = passed_along(echo_rows, "vox", -1)
    kept = echo_rows.shape[0]
    lower_part = echo_rows.reshape(kept, BLOCK_CH, frames, WINDOW)
    upper_part = upper_rows.reshape(kept, BLOCK_CH, frames, WINDOW)
    extended = jnp.concatenate([lower_part, upper_part], axis=3)
    windows = jax.vmap(jax.vmap(take_window))(extended, block_delays)
    summed = (
        jnp.sum(windows.astype(jnp.float32), axis=1) * own_gates.astype(jnp.float32)[:, None, None]
    )
    summed_blocks = summed.astype(jnp.bfloat16)
    own_geometry = (
        lax.dynamic_index_in_dim(offset_table, group, 0, keepdims=False),
        lax.dynamic_index_in_dim(slope_table, group, 0, keepdims=False),
        lax.dynamic_index_in_dim(tilt_table, group, 0, keepdims=False),
    )
    partial_value = project(summed_blocks, own_geometry, 0, SLAB_VOX)
    beam = lax.psum_scatter(
        partial_value.astype(jnp.bfloat16), "chan", scatter_dimension=1, tiled=True
    ).astype(jnp.float32)
    local_gram = jnp.dot(beam, beam.T, precision=lax.Precision.HIGHEST)
    gram_matrix = lax.psum(local_gram, ("chan", "vox"))
    basis = refine_basis(gram_matrix, prior_basis)
    coefficients = jnp.dot(basis.T, beam, precision=lax.Precision.HIGHEST)
    clean = beam - jnp.dot(basis, coefficients, precision=lax.Precision.HIGHEST)
    power = jnp.sum(clean * clean, axis=0) / FRAMES
    return power.reshape(1, -1)


def solution(mesh):
    in_specs = (
        P("chan", "vox", None),
        P("chan", "vox"),
        P(),
        P(None, "vox"),
        P(None, "vox"),
        P(None, "vox"),
        P(),
    )
    out_specs = P("vox", "chan")
    return jax.shard_map(body, mesh=mesh, in_specs=in_specs, out_specs=out_specs, check_vma=False)
```

profile of v0, /device:TPU:1, one launch (start us, length us, event | category | flops | bytes accessed | tf_op | source)
XLA Modules:
  0.0 315.6 jit_solution(16673439576593930064)
XLA Ops:
  6.5 5.2 %collective-permute-start = (bf16[32,8,6400]{2,1,0:T(8,128)(2,1)}, bf16[32,8,6400]{2,1,0:T(8,128)(2,1)S(1)}, u32[]{:S(2)}, u32[]{:S(2)}) collective-permute-start(bf16[32,8,6400]{2,1,0:T(8,128)(2,1)} %bitcast.74), channel_id=1, source_target_pairs={{1,0},{2,1},{3,2},{4,3},{5,4},{6,5},{7,6},{8,7},{9,8},{10,9},{11,1... | collective-permute-start | bytes 9830408 | tf_op jit(solution)/shard_map/ppermute | solution.py:19
  11.8 9.1 %reshape_reshape.3 = bf16[32,8,100,64]{3,2,1,0:T(8,128)(2,1)} reshape(bf16[256,1,6400]{2,0,1:T(8,128)(2,1)} %param.12) | data formatting | bytes 6553600 | tf_op jit(solution)/shard_map/reshape;reshape | solution.py:86
  22.5 10.2 %copy.14 = bf16[32,8,100,64]{2,1,0,3:T(8,128)(2,1)} copy(bf16[32,8,100,64]{3,2,1,0:T(8,128)(2,1)} %reshape_reshape.3) | data formatting | bytes 6553600 | tf_op jit(solution)/shard_map/reshape;reshape | solution.py:86
  35.9 12.3 %collective-permute-done = bf16[32,8,6400]{2,1,0:T(8,128)(2,1)S(1)} collective-permute-done((bf16[32,8,6400]{2,1,0:T(8,128)(2,1)}, bf16[32,8,6400]{2,1,0:T(8,128)(2,1)S(1)}, u32[]{:S(2)}, u32[]{:S(2)}) %collective-permute-start) | collective-permute-done | bytes 3276832 | tf_op jit(solution)/shard_map/ppermute | solution.py:19
  48.1 6.8 %reshape.189 = bf16[32,8,100,64]{3,2,1,0:T(8,128)(2,1)} reshape(bf16[32,8,6400]{2,1,0:T(8,128)(2,1)S(1)} %collective-permute-done) | data formatting | bytes 6553600 | tf_op jit(solution)/shard_map/reshape | solution.py:87
  54.9 10.2 %copy.15 = bf16[32,8,100,64]{2,1,0,3:T(8,128)(2,1)} copy(bf16[32,8,100,64]{3,2,1,0:T(8,128)(2,1)} %reshape.189) | data formatting | bytes 6553600 | tf_op jit(solution)/shard_map/reshape | solution.py:87
  65.1 8.3 %pad_maximum_fusion = bf16[32,8,100,128]{2,1,0,3:T(8,128)(2,1)} fusion(bf16[32,8,100,64]{2,1,0,3:T(8,128)(2,1)} %copy.15, bf16[32,8,100,64]{2,1,0,3:T(8,128)(2,1)} %copy.14), kind=kLoop, calls=%fused_computation.35 | loop fusion | flops 3276800 | bytes 13107200 | tf_op jit(solution)/shard_map/concatenate | solution.py:88
  73.4 18.5 %gather_fusion = bf16[256,100,64]{1,0,2:T(8,128)(2,1)} fusion(bf16[32,8,100,128]{2,1,0,3:T(8,128)(2,1)} %pad_maximum_fusion, s32[256]{0:T(256)S(1)} %reshape.194), kind=kCustom, calls=%fused_computation | custom fusion | bytes 6557696 | tf_op jit(solution)/shard_map/vmap(vmap())/gather | solution.py:35
  91.9 4.9 %convert_reduce_fusion = f32[32,100,64]{1,0,2:T(8,128)S(1)} fusion(bf16[256,100,64]{1,0,2:T(8,128)(2,1)} %gather_fusion), kind=kLoop, calls=%fused_computation.36 | loop fusion | flops 3072000 | bytes 4096000 | tf_op jit(solution)/shard_map/reduce_sum | solution.py:91
  97.5 63.0 %while.13 = (s32[]{:T(128)}, f32[100,16384]{1,0:T(8,128)}, bf16[8,4,100,64]{2,3,1,0:T(8,128)(2,1)S(1)}, f32[8,4]{1,0:T(8,128)S(1)}, f32[8,4]{1,0:T(8,128)S(1)}, /*index=5*/f32[8,4]{1,0:T(8,128)S(1)}, s32[]{:T(128)}, s32[]{:T(128)}) while((s32[]{:T(128)}, f32[100,16384]{1,0:T(8,128)}, bf16[8,4,100,64]{2,3,1,0:T(8,128)(2,1)S(1)}, ...), condition=%wide.region_2.3_spmd.clone, body=%wide.region_1.2_spmd.clone.sunk | while | flops 867795008 | bytes 13960187 | solution.py:65
  97.7 6.0 %fusion.75 = f32[100,16384]{1,0:T(8,128)} fusion(f32[4,16384]{1,0:T(4,128)S(1)} %multiply_add_fusion.2, f32[64]{0:T(128)S(1)} %iota_convert_fusion.2, f32[100,16384]{1,0:T(8,128)} %get-tuple-element.183, pred[]{:T(512)S(6)} %compare.17, bf16[8,4,100,64]{2,3,1,0:T(8,128)(2,1)S(1)} %get-tuple-element.192, s32[]{:T(128)} %get-tuple-element.182), kind=kOutput, calls=%fused_computation.2.clone.1 | convolution fusion | flops 867303424 | bytes 13435397 | tf_op jit(solution)/shard_map/while/body/eval_jaxpr/bfk,bkv->fv/dot_general | solution.py:61
  103.9 7.9 %fusion.75 = f32[100,16384]{1,0:T(8,128)} fusion(f32[4,16384]{1,0:T(4,128)S(1)} %multiply_add_fusion.2, f32[64]{0:T(128)S(1)} %iota_convert_fusion.2, f32[100,16384]{1,0:T(8,128)} %get-tuple-element.183, pred[]{:T(512)S(6)} %compare.17, bf16[8,4,100,64]{2,3,1,0:T(8,128)(2,1)S(1)} %get-tuple-element.192, s32[]{:T(128)} %get-tuple-element.182), kind=kOutput, calls=%fused_computation.2.clone.1 | convolution fusion | flops 867303424 | bytes 13435397 | tf_op jit(solution)/shard_map/while/body/eval_jaxpr/bfk,bkv->fv/dot_general | solution.py:61
  112.0 7.9 %fusion.75 = f32[100,16384]{1,0:T(8,128)} fusion(f32[4,16384]{1,0:T(4,128)S(1)} %multiply_add_fusion.2, f32[64]{0:T(128)S(1)} %iota_convert_fusion.2, f32[100,16384]{1,0:T(8,128)} %get-tuple-element.183, pred[]{:T(512)S(6)} %compare.17, bf16[8,4,100,64]{2,3,1,0:T(8,128)(2,1)S(1)} %get-tuple-element.192, s32[]{:T(128)} %get-tuple-element.182), kind=kOutput, calls=%fused_computation.2.clone.1 | convolution fusion | flops 867303424 | bytes 13435397 | tf_op jit(solution)/shard_map/while/body/eval_jaxpr/bfk,bkv->fv/dot_general | solution.py:61
  120.1 7.9 %fusion.75 = f32[100,16384]{1,0:T(8,128)} fusion(f32[4,16384]{1,0:T(4,128)S(1)} %multiply_add_fusion.2, f32[64]{0:T(128)S(1)} %iota_convert_fusion.2, f32[100,16384]{1,0:T(8,128)} %get-tuple-element.183, pred[]{:T(512)S(6)} %compare.17, bf16[8,4,100,64]{2,3,1,0:T(8,128)(2,1)S(1)} %get-tuple-element.192, s32[]{:T(128)} %get-tuple-element.182), kind=kOutput, calls=%fused_computation.2.clone.1 | convolution fusion | flops 867303424 | bytes 13435397 | tf_op jit(solution)/shard_map/while/body/eval_jaxpr/bfk,bkv->fv/dot_general | solution.py:61
  128.2 7.9 %fusion.75 = f32[100,16384]{1,0:T(8,128)} fusion(f32[4,16384]{1,0:T(4,128)S(1)} %multiply_add_fusion.2, f32[64]{0:T(128)S(1)} %iota_convert_fusion.2, f32[100,16384]{1,0:T(8,128)} %get-tuple-element.183, pred[]{:T(512)S(6)} %compare.17, bf16[8,4,100,64]{2,3,1,0:T(8,128)(2,1)S(1)} %get-tuple-element.192, s32[]{:T(128)} %get-tuple-element.182), kind=kOutput, calls=%fused_computation.2.clone.1 | convolution fusion | flops 867303424 | bytes 13435397 | tf_op jit(solution)/shard_map/while/body/eval_jaxpr/bfk,bkv->fv/dot_general | solution.py:61
  136.4 7.9 %fusion.75 = f32[100,16384]{1,0:T(8,128)} fusion(f32[4,16384]{1,0:T(4,128)S(1)} %multiply_add_fusion.2, f32[64]{0:T(128)S(1)} %iota_convert_fusion.2, f32[100,16384]{1,0:T(8,128)} %get-tuple-element.183, pred[]{:T(512)S(6)} %compare.17, bf16[8,4,100,64]{2,3,1,0:T(8,128)(2,1)S(1)} %get-tuple-element.192, s32[]{:T(128)} %get-tuple-element.182), kind=kOutput, calls=%fused_computation.2.clone.1 | convolution fusion | flops 867303424 | bytes 13435397 | tf_op jit(solution)/shard_map/while/body/eval_jaxpr/bfk,bkv->fv/dot_general | solution.py:61
  144.5 7.9 %fusion.75 = f32[100,16384]{1,0:T(8,128)} fusion(f32[4,16384]{1,0:T(4,128)S(1)} %multiply_add_fusion.2, f32[64]{0:T(128)S(1)} %iota_convert_fusion.2, f32[100,16384]{1,0:T(8,128)} %get-tuple-element.183, pred[]{:T(512)S(6)} %compare.17, bf16[8,4,100,64]{2,3,1,0:T(8,128)(2,1)S(1)} %get-tuple-element.192, s32[]{:T(128)} %get-tuple-element.182), kind=kOutput, calls=%fused_computation.2.clone.1 | convolution fusion | flops 867303424 | bytes 13435397 | tf_op jit(solution)/shard_map/while/body/eval_jaxpr/bfk,bkv->fv/dot_general | solution.py:61
  152.6 7.9 %fusion.75 = f32[100,16384]{1,0:T(8,128)} fusion(f32[4,16384]{1,0:T(4,128)S(1)} %multiply_add_fusion.2, f32[64]{0:T(128)S(1)} %iota_convert_fusion.2, f32[100,16384]{1,0:T(8,128)} %get-tuple-element.183, pred[]{:T(512)S(6)} %compare.17, bf16[8,4,100,64]{2,3,1,0:T(8,128)(2,1)S(1)} %get-tuple-element.192, s32[]{:T(128)} %get-tuple-element.182), kind=kOutput, calls=%fused_computation.2.clone.1 | convolution fusion | flops 867303424 | bytes 13435397 | tf_op jit(solution)/shard_map/while/body/eval_jaxpr/bfk,bkv->fv/dot_general | solution.py:61
  160.5 5.0 %convert_element_type.63 = bf16[100,16384]{1,0:T(8,128)(2,1)} convert(f32[100,16384]{1,0:T(8,128)} %get-tuple-element.87) | non-fusion elementwise | flops 1638400 | bytes 9830400 | tf_op jit(solution)/shard_map/convert_element_type | solution.py:101
  165.6 45.8 %reduce-scatter.2.cloned.1.call-done = bf16[100,4096]{1,0:T(8,128)(2,1)} async-done(((bf16[100,16384]{1,0:T(8,128)(2,1)}), bf16[100,4096]{1,0:T(8,128)(2,1)}) %reduce-scatter.2.cloned.1.call-update) | async-done | bytes 819216 | tf_op jit(solution)/shard_map/reduce_scatter | solution.py:100
  213.2 76.4 %psum.7 = f32[100,100]{1,0:T(8,128)S(1)} all-reduce(f32[100,100]{1,0:T(8,128)S(1)} %fusion.46), channel_id=1, replica_groups=mesh['chan'=4,'vox'=64] {'chan','vox'}, use_global_device_ids=true, to_apply=%region_4.5 | all-reduce | flops 10000 | bytes 80000 | tf_op jit(solution)/shard_map/psum | solution.py:104
  290.0 2.7 cholesky.44
  297.1 2.7 cholesky.55
  305.3 2.8 fusion.23
  (97 shorter events, 19.4 us)
Async XLA Ops:
  6.5 14.4 %copy-start = (s32[128,64]{0,1:T(8,128)S(1)}, s32[128,64]{0,1:T(8,128)}, u32[]{:S(2)}) copy-start(s32[128,64]{0,1:T(8,128)} %param.14) | copy-start | bytes 98308
  6.5 15.1 %copy-start.3 = (f32[128,1]{0,1:T(1,128)S(1)}, f32[128,1]{0,1:T(1,128)}, u32[]{:S(2)}) copy-start(f32[128,1]{0,1:T(1,128)} %param.15) | copy-start | bytes 1540
  6.5 204.8 %reduce-scatter.2.cloned.1.call-start = ((), (), s32[]{:S(2)}) async-start(), calls=%async_computation.1 | async-start | bytes 4259840 | tf_op jit(solution)/shard_map/reduce_scatter | solution.py:100
  6.5 41.6 %collective-permute-start = (bf16[32,8,6400]{2,1,0:T(8,128)(2,1)}, bf16[32,8,6400]{2,1,0:T(8,128)(2,1)S(1)}, u32[]{:S(2)}, u32[]{:S(2)}) collective-permute-start(bf16[32,8,6400]{2,1,0:T(8,128)(2,1)} %bitcast.74), channel_id=1, source_target_pairs={{1,0},{2,1},{3,2},{4,3},{5,4},{6,5},{7,6},{8,7},{9,8},{10,9},{11,1... | collective-permute-start | bytes 9830408 | tf_op jit(solution)/shard_map/ppermute | solution.py:19
  20.9 12.3 %copy-start.2 = (s32[256,1]{0,1:T(1,128)S(1)}, s32[256,1]{0,1:T(1,128)}, u32[]{:S(2)}) copy-start(s32[256,1]{0,1:T(1,128)} %param.13) | copy-start | bytes 3076
  20.9 13.2 %copy-start.4 = (f32[128,1]{0,1:T(1,128)S(1)}, f32[128,1]{0,1:T(1,128)}, u32[]{:S(2)}) copy-start(f32[128,1]{0,1:T(1,128)} %param.16) | copy-start | bytes 1540
  20.9 14.0 %copy-start.5 = (f32[128,1]{0,1:T(1,128)S(1)}, f32[128,1]{0,1:T(1,128)}, u32[]{:S(2)}) copy-start(f32[128,1]{0,1:T(1,128)} %param.17) | copy-start | bytes 1540
  160.5 129.1 %copy-start.1 = (f32[100,30]{0,1:T(8,128)S(1)}, f32[100,30]{0,1:T(8,128)}, u32[]{:S(2)}) copy-start(f32[100,30]{0,1:T(8,128)} %param.18) | copy-start | bytes 36004
Sparse Core Ops, SparseCore 0:
  165.7 45.6 reduce-scatter.1
where the time goes:
time: 317 us; the launch traced here: 316 us
  blocking collectives  76.4 us (24%)
  matrix products  68.8 us (22%)
  waiting for transfers between devices  58.1 us (18%)
  local copies, waits for them, and re-layouts  57 us (18%)
  other arithmetic  36.3 us (11%)
  between operations  13.6 us (4%)
  starting transfers between devices  5.23 us (2%)
    psum x1, blocking collectives, body(): gram_matrix = lax.psum(local_gram, ('chan', 'vox'))  76.4 us
    dot_general x8, matrix products, one_turn(): jnp.einsum('bfk,bkv->fv', pieces[0], table, preferred_element_type=jnp.fl...  61.4 us
    reduce_scatter x1, waiting for transfers between devices, body(): lax.psum_scatter(partial_value.astype(jnp.bfloat16), 'chan', scatter_dime...  45.8 us
    another operation x2, local copies, waits for them, and re-layouts, body(): lower_part = echo_rows.reshape(kept, BLOCK_CH, frames, WINDOW)  19.3 us
    gather x2, local copies, waits for them, and re-layouts, take_window(): lax.dynamic_slice(row, (jnp.zeros((), jnp.int32), start), (row.shape[0],...  18.6 us
    reshape x2, local copies, waits for them, and re-layouts, body(): upper_part = upper_rows.reshape(kept, BLOCK_CH, frames, WINDOW)  17 us
    ppermute x1, waiting for transfers between devices, passed_along(): return lax.ppermute(block, axis, route)  12.3 us
    concatenate x1, other arithmetic, body(): extended = jnp.concatenate([lower_part, upper_part], axis=3)  8.31 us
  transfers between devices with their start and end apart: 2, of which 2 were waited for; matrix products, arithmetic and copies ran while one was open for 8% of the time, Pallas kernels for 0%

commit v1 on v0

v1 whole, which is shorter than its diff:
```python
import functools

import jax
import jax.numpy as jnp
from jax import lax
from jax.experimental import pallas as pl
from jax.experimental.pallas import tpu as pltpu
from jax.sharding import PartitionSpec as P

MESH = pl.DeviceIdType.MESH
FRAMES = 100
RANK = 30
PAIRS = 50
ROWS = 64
RUN = 16
GROUP = 32
SLABS = 64
BAND = 32
VMEM = pltpu.VMEM
F32 = jnp.float32
BF16 = jnp.bfloat16


def iota(shape, dim):
    return lax.broadcasted_iota(jnp.int32, shape, dim)


def active_run(row, group):
    lane = iota(row.shape, 1)
    before = jnp.where(lane % GROUP == 0, pltpu.roll(row, 97, 1), pltpu.roll(row, 1, 1))
    mine = (lane // GROUP == group).astype(jnp.int32)
    first = (row * (1 - before) * mine * (lane % GROUP)).astype(F32)
    start = jnp.sum(first).astype(jnp.int32)
    count = jnp.sum((row * mine).astype(F32)).astype(jnp.int32)
    return start, count


def window_kernel(own, aperture_ref, delay_ref, echo_ref, out_ref, moved_ref, rows_ref):
    group = lax.axis_index("chan")
    slab = lax.axis_index("vox")
    if not own:
        slab = lax.rem(slab + SLABS - 1, SLABS)
    row = aperture_ref[pl.ds(slab, 1), :]
    start, count = active_run(row, group)
    lane = iota((8, 128), 1)
    sub = iota((8, 128), 0)
    sample = lane & 63
    low = jnp.broadcast_to(delay_ref[0:1, 0:128], (8, 128))
    high = jnp.broadcast_to(delay_ref[0:1, 128:256], (8, 128))

    def pair(i, carry):
        blocks, picks, keeps = [], [], []
        for q in range(2):
            block = lax.rem(start + 2 * i + q, GROUP)
            table = jnp.where(block < 16, low, high)
            delay = jnp.take_along_axis(table, (block & 15) * 8 + sub, axis=1)
            if own:
                picks.append((lane + delay) & 127)
                keeps.append(sample + delay < 64)
            else:
                picks.append((lane + delay + 64) & 127)
                keeps.append(sample + delay >= 64)
            blocks.append(block)
        for t in range(PAIRS):
            parts = []
            for q in range(2):
                values = echo_ref[blocks[q], :, t * 128 : (t + 1) * 128].astype(F32)
                values = jnp.take_along_axis(values, picks[q], axis=1)
                parts.append(jnp.where(keeps[q], values, 0.0))
            moved_ref[pl.ds(i * 16, 16), t * 128 : (t + 1) * 128] = jnp.concatenate(
                parts, axis=0
            ).astype(BF16)
        return carry

    lax.fori_loop(0, RUN // 2, pair, 0)
    rows_ref[...] = jnp.zeros_like(rows_ref)
    block_of = iota((RUN, 128), 0)
    gather = (iota((RUN, 128), 1) // 8 == block_of) & (block_of < count)
    gather = jnp.where(gather, 1.0 / 32, 0.0).astype(BF16)
    for c in range(PAIRS // 2):
        sums = jnp.dot(
            gather, moved_ref[:, c * 256 : (c + 1) * 256], preferred_element_type=F32
        )
        for q in range(2):
            for h in range(2):
                rows_ref[pl.ds(h * 8 * ROWS + 2 * c + q, 8, stride=ROWS), :] = sums[
                    h * 8 : h * 8 + 8, q * 128 : (q + 1) * 128
                ]
    out_ref[...] = rows_ref[...].astype(out_ref.dtype)


def window_sums(own, aperture, delay, echo):
    return pl.pallas_call(
        functools.partial(window_kernel, own),
        out_shape=jax.ShapeDtypeStruct((RUN * ROWS, 128), F32 if own else BF16),
        in_specs=[pl.BlockSpec(memory_space=VMEM)] * 3,
        out_specs=pl.BlockSpec(memory_space=VMEM),
        scratch_shapes=[VMEM((128, 128 * PAIRS), BF16), VMEM((RUN * ROWS, 128), F32)],
        name="window_own" if own else "window_prev",
        cost_estimate=pl.CostEstimate(flops=10**8, bytes_accessed=4 * 10**6, transcendentals=0),
    )(aperture, delay, echo)


def share_kernel(own_ref, prev_ref, out_ref, next_ref, all_ref, send, recv, peer_send, peer_recv):
    group = lax.axis_index("chan")
    slab = lax.axis_index("vox")
    before = lax.rem(slab + SLABS - 1, SLABS)
    after = lax.rem(slab + 1, SLABS)
    peers = [lax.rem(group + d, 4) for d in range(1, 4)]
    barrier = pltpu.get_barrier_semaphore()
    for place in [(group, before), (group, after)] + [(p, slab) for p in peers]:
        pl.semaphore_signal(barrier, inc=1, device_id=place, device_id_type=MESH)
    pl.semaphore_wait(barrier, 5)
    copy = pltpu.make_async_remote_copy(
        src_ref=prev_ref,
        dst_ref=next_ref,
        send_sem=send,
        recv_sem=recv,
        device_id=(group, before),
        device_id_type=MESH,
    )
    copy.start()
    copy.wait()
    live = jnp.where(slab < SLABS - 1, 1.0, 0.0)
    size = RUN * ROWS
    all_ref[pl.ds(pl.multiple_of(group * size, size), size), :] = (
        own_ref[...] + next_ref[...].astype(F32) * live
    ).astype(BF16)
    here = all_ref.at[pl.ds(pl.multiple_of(group * size, size), size), :]
    copies = []
    for d in range(3):
        copies.append(
            pltpu.make_async_remote_copy(
                src_ref=here,
                dst_ref=here,
                send_sem=peer_send.at[d],
                recv_sem=peer_recv.at[d],
                device_id=(peers[d], slab),
                device_id_type=MESH,
            )
        )
    for c in copies:
        c.start()
    for c in copies:
        c.wait()
    out_ref[...] = all_ref[...]


def share(own, prev):
    return pl.pallas_call(
        share_kernel,
        out_shape=jax.ShapeDtypeStruct((4 * RUN * ROWS, 128), BF16),
        in_specs=[pl.BlockSpec(memory_space=VMEM)] * 2,
        out_specs=pl.BlockSpec(memory_space=VMEM),
        scratch_shapes=[
            VMEM((RUN * ROWS, 128), BF16),
            VMEM((4 * RUN * ROWS, 128), BF16),
            pltpu.SemaphoreType.DMA,
            pltpu.SemaphoreType.DMA,
            pltpu.SemaphoreType.DMA((3,)),
            pltpu.SemaphoreType.DMA((3,)),
        ],
        compiler_params=pltpu.CompilerParams(collective_id=0, has_side_effects=True),
        name="share",
    )(own, prev)


def project_kernel(
    aperture_ref, offset_ref, slope_ref, tilt_ref, all_ref, beam_ref, gram_ref, lhs_ref, geo_ref
):
    group = lax.axis_index("chan")
    slab = lax.axis_index("vox")
    row = aperture_ref[pl.ds(slab, 1), :]
    lane8 = iota((8, 128), 1)
    slot = lane8 // BAND
    for g in range(4):
        start, _ = active_run(row, g)

        def quad(q, carry):
            sums = [[[None] * 8 for par in range(2)] for h in range(2)]
            for k in range(4):
                j = q * 4 + k
                block = g * GROUP + lax.rem(start + j, GROUP)
                offset = offset_ref[0, block]
                tilt = tilt_ref[0, block]
                place = g * RUN + j
                geo_ref[2, place] = slope_ref[0, block]
                geo_ref[3, place] = tilt
                picks = []
                for h in range(2):
                    origin = offset + tilt * (64 * group + 32 * h).astype(F32)
                    first = origin.astype(jnp.int32)
                    geo_ref[h, place] = origin - first.astype(F32)
                    picks.append(first + (lane8 & (BAND - 1)))
                base = pl.multiple_of(place * ROWS, ROWS)
                for r in range(4):
                    part = all_ref[pl.ds(base + r * 16, 16), :].astype(F32)
                    for half in range(2):
                        values = part[half * 8 : half * 8 + 8]
                        for h in range(2):
                            for par in range(2):
                                got = jnp.take_along_axis(
                                    values, (picks[h] + 64 * par) & 127, axis=1
                                )
                                old = sums[h][par][2 * r + half]
                                sums[h][par][2 * r + half] = (
                                    got if old is None else jnp.where(slot == k, got, old)
                                )
            for h in range(2):
                for par in range(2):
                    lhs_ref[
                        h,
                        par * ROWS : (par + 1) * ROWS,
                        pl.ds(pl.multiple_of((g * 4 + q) * 128, 128), 128),
                    ] = jnp.concatenate(sums[h][par], axis=0).astype(BF16)
            return carry

        lax.fori_loop(0, 4, quad, 0)

    gram_ref[...] = jnp.zeros_like(gram_ref)
    depth = (lane8 & 63).astype(F32)
    band = iota((8, 128), 0).astype(F32)

    for h in range(2):

        def tile(n, carry):
            total = jnp.zeros((128, 256), F32)
            for c in range(8):
                rows = []
                for b in range(8):
                    place = c * 8 + b
                    origin = geo_ref[h, place]
                    slope = geo_ref[2, place]
                    tilt = geo_ref[3, place]
                    columns = []
                    for i in range(2):
                        lateral = ((lane8 >> 6) + 2 * i + 4 * n).astype(F32)
                        position = origin + slope * depth + tilt * lateral
                        parts = [
                            jnp.maximum(0.0, 1.0 - jnp.abs(band + (8.0 * k) - position))
                            for k in range(4)
                        ]
                        columns.append(jnp.concatenate(parts, axis=0).astype(BF16))
                    rows.append(jnp.concatenate(columns, axis=1))
                table = jnp.concatenate(rows, axis=0)
                total = total + jnp.dot(
                    lhs_ref[h, :, c * 256 : (c + 1) * 256], table, preferred_element_type=F32
                )
            high = total.astype(BF16)
            low = (total - high.astype(F32)).astype(BF16)
            both = jnp.concatenate([high, low], axis=0)
            beam_ref[:, pl.ds(pl.multiple_of((h * 8 + n) * 256, 256), 256)] = both
            gram_ref[...] += lax.dot_general(
                both, both, (((1,), (1,)), ((), ())), preferred_element_type=F32
            )
            return carry

        lax.fori_loop(0, 8, tile, 0)


def project(aperture, offset, slope, tilt, everything):
    smem = pl.BlockSpec(memory_space=pltpu.SMEM)
    vmem = pl.BlockSpec(memory_space=VMEM)
    beam, gram = pl.pallas_call(
        project_kernel,
        out_shape=(
            jax.ShapeDtypeStruct((256, 4096), BF16),
            jax.ShapeDtypeStruct((256, 256), F32),
        ),
        in_specs=[vmem, smem, smem, smem, vmem],
        out_specs=(vmem, vmem),
        scratch_shapes=[VMEM((2, 128, 64 * BAND), BF16), pltpu.SMEM((4, 64), F32)],
        name="project",
    )(aperture, offset, slope, tilt, everything)
    return beam, gram


def sweep(gram, rows):
    product = jnp.dot(rows, gram, precision=lax.Precision.HIGHEST, preferred_element_type=F32)
    normal = lax.dot_general(
        product,
        product,
        (((1,), (1,)), ((), ())),
        precision=lax.Precision.HIGHEST,
        preferred_element_type=F32,
    )
    normal = jnp.concatenate([normal, jnp.zeros((32, 96), F32)], axis=1)
    sub = iota((32, 128), 0)
    scale = jnp.zeros((32, 128), F32)
    for j in range(RANK):
        column = jnp.take_along_axis(normal, jnp.full((32, 128), j, jnp.int32), axis=1)
        pivot = jnp.broadcast_to(column[j : j + 1], (32, 128))
        scale = jnp.where(sub == j, lax.rsqrt(pivot), scale)
        factor = jnp.where(sub > j, column / pivot, 0.0)
        normal = normal - factor * normal[j : j + 1]
        product = product - factor * product[j : j + 1]
    return product * scale


def filter_kernel(gram_ref, prior_ref, beam_ref, out_ref):
    gram = gram_ref[...]
    lane = iota((32, 128), 1)
    pick = jnp.minimum(2 * (lane & 63) + (lane >> 6), 127)
    rows = jnp.take_along_axis(prior_ref[...], pick, axis=1)
    rows = jnp.where((lane & 63) < PAIRS, rows, 0.0)
    rows = sweep(gram, rows)
    rows = sweep(gram, rows)
    overlap = lax.dot_general(
        rows,
        rows,
        (((0,), (0,)), ((), ())),
        precision=lax.Precision.HIGHEST,
        preferred_element_type=F32,
    )
    keep = jnp.where(iota((128, 128), 0) == iota((128, 128), 1), 1.0, 0.0) - overlap
    high = keep.astype(BF16)
    low = (keep - high.astype(F32)).astype(BF16)
    twice = jnp.concatenate([high, high], axis=1)
    for c in range(16):
        beam = beam_ref[:, c * 256 : (c + 1) * 256]
        clean = jnp.dot(twice, beam, preferred_element_type=F32)
        clean = clean + jnp.dot(low, beam[0:128], preferred_element_type=F32)
        out_ref[:, c * 256 : (c + 1) * 256] = jnp.sum(
            clean * clean, axis=0, keepdims=True
        ) * (1.0 / FRAMES)


def combine_kernel(wide_ref, out_ref, mine_ref, got_ref, sum_ref, all_ref, send, recv):
    group = lax.axis_index("chan")
    slab = lax.axis_index("vox")
    core = lax.rem(slab, 2)
    chip = slab // 2
    y, z = chip // 8, lax.rem(chip, 8)
    me = group * 2 + core
    around = []
    for d in range(1, 8):
        peer = lax.rem(me + d, 8)
        around.append((peer, (peer // 2, slab - core + lax.rem(peer, 2))))
    along_y = [(group, (lax.rem(y + d, 4) * 8 + z) * 2 + core) for d in range(1, 4)]
    along_z = [(group, (y * 8 + lax.rem(z + d, 8)) * 2 + core) for d in range(1, 8)]
    barrier = pltpu.get_barrier_semaphore()
    for place in [a[1] for a in around] + along_y + along_z:
        pl.semaphore_signal(barrier, inc=1, device_id=place, device_id_type=MESH)
    mine_ref[...] = (
        wide_ref[0:128, 0:128]
        + wide_ref[128:256, 0:128]
        + wide_ref[0:128, 128:256]
        + wide_ref[128:256, 128:256]
    )
    pl.semaphore_wait(barrier, 17)

    def copy(src, dst, place, k):
        return pltpu.make_async_remote_copy(
            src_ref=src,
            dst_ref=dst,
            send_sem=send.at[k],
            recv_sem=recv.at[k],
            device_id=place,
            device_id_type=MESH,
        )

    def rows(k):
        return pl.ds(pl.multiple_of(k * 16, 16), 16)

    copies = [
        copy(mine_ref.at[rows(peer)], got_ref.at[k], place, k)
        for k, (peer, place) in enumerate(around)
    ]
    for c in copies:
        c.start()
    for c in copies:
        c.wait()
    total = mine_ref[rows(me), :]
    for k in range(7):
        total = total + got_ref[k]
    sum_ref[0] = total
    copies = [copy(sum_ref.at[0], got_ref.at[7 + k], p, 7 + k) for k, p in enumerate(along_y)]
    for c in copies:
        c.start()
    for c in copies:
        c.wait()
    for k in range(3):
        total = total + got_ref[7 + k]
    sum_ref[1] = total
    copies = [copy(sum_ref.at[1], got_ref.at[10 + k], p, 10 + k) for k, p in enumerate(along_z)]
    for c in copies:
        c.start()
    for c in copies:
        c.wait()
    for k in range(7):
        total = total + got_ref[10 + k]
    here = all_ref.at[rows(me), :]
    all_ref[rows(me), :] = total
    copies = [copy(here, here, place, 17 + k) for k, (_, place) in enumerate(around)]
    for c in copies:
        c.start()
    for c in copies:
        c.wait()
    out_ref[...] = all_ref[...]


def combine(gram):
    return pl.pallas_call(
        combine_kernel,
        out_shape=jax.ShapeDtypeStruct((128, 128), F32),
        in_specs=[pl.BlockSpec(memory_space=VMEM)],
        out_specs=pl.BlockSpec(memory_space=VMEM),
        scratch_shapes=[
            VMEM((128, 128), F32),
            VMEM((17, 16, 128), F32),
            VMEM((2, 16, 128), F32),
            VMEM((128, 128), F32),
            pltpu.SemaphoreType.DMA((24,)),
            pltpu.SemaphoreType.DMA((24,)),
        ],
        compiler_params=pltpu.CompilerParams(collective_id=1, has_side_effects=True),
        name="combine",
    )(gram)


def body(echo_data, delays, aperture, offset, depth_slope, lateral_tilt, prior_basis):
    echo = echo_data.reshape(32, 8, 6400)
    delay = delays.reshape(1, 256)
    own_aperture = aperture.T
    prev_delay = lax.ppermute(delay, "vox", [(i, (i + 1) % SLABS) for i in range(SLABS)])
    own = window_sums(True, own_aperture, delay, echo)
    prev = window_sums(False, own_aperture, prev_delay, echo)
    everything = share(own, prev)
    beam, gram = project(
        own_aperture,
        offset.reshape(1, 128),
        depth_slope.reshape(1, 128),
        lateral_tilt.reshape(1, 128),
        everything,
    )
    gram = combine(gram)
    prior = jnp.pad(prior_basis.T, ((0, 32 - RANK), (0, 128 - FRAMES)))
    vmem = pl.BlockSpec(memory_space=VMEM)
    return pl.pallas_call(
        filter_kernel,
        out_shape=jax.ShapeDtypeStruct((1, 4096), F32),
        in_specs=[vmem] * 3,
        out_specs=vmem,
        name="filter",
    )(gram, prior, beam)


def solution(mesh):
    in_specs = (
        P("chan", "vox", None),
        P("chan", "vox"),
        P(),
        P(None, "vox"),
        P(None, "vox"),
        P(None, "vox"),
        P(),
    )
    out_specs = P("vox", "chan")
    return jax.shard_map(body, mesh=mesh, in_specs=in_specs, out_specs=out_specs, check_vma=False)
```

time: 317 us -> 90.4 us (0.29)
  Pallas kernels: 0 us -> 85.9 us
  blocking collectives: 76.4 us -> 0 us
  matrix products: 68.8 us -> 0 us
  waiting for transfers between devices: 58.1 us -> 0.01 us
  local copies, waits for them, and re-layouts: 57 us -> 1.17 us
  other arithmetic: 36.3 us -> 0 us
  between operations: 13.6 us -> 0.02 us
    pallas_call x0 -> x6, Pallas kernels: none -> 85.9 us  [the longest x1 26.3 us: combine(): pl.pallas_call(combine_kernel, out_shape=jax.ShapeDtypeStruct((128, 128),...]
    psum x1 -> x0, blocking collectives: 76.4 us -> none  [body(): gram_matrix = lax.psum(local_gram, ('chan', 'vox'))]
    dot_general x15 -> x0, matrix products: 68.3 us -> none  [the longest x8 61.4 us: one_turn(): jnp.einsum('bfk,bkv->fv', pieces[0], table, preferred_element_type=jnp.fl...]
    reduce_scatter x1 -> x0, waiting for transfers between devices: 45.8 us -> none  [body(): lax.psum_scatter(partial_value.astype(jnp.bfloat16), 'chan', scatter_dime...]
    another operation x6 -> x0, local copies, waits for them, and re-layouts: 19.6 us -> none  [the longest x2 19.3 us: body(): lower_part = echo_rows.reshape(kept, BLOCK_CH, frames, WINDOW)]
    gather x2 -> x0, local copies, waits for them, and re-layouts: 18.6 us -> none  [take_window(): lax.dynamic_slice(row, (jnp.zeros((), jnp.int32), start), (row.shape[0],...]
    reshape x6 -> x0, local copies, waits for them, and re-layouts: 17.3 us -> none  [the longest x2 17 us: body(): upper_part = upper_rows.reshape(kept, BLOCK_CH, frames, WINDOW)]
    another operation x10 -> x0, other arithmetic: 12.7 us -> none  [the longest x6 6.84 us: refine_basis(): factor = jnp.linalg.cholesky(normal_matrix)]
  transfers between devices with their start and end apart: 2 -> 1, of which waited for: 2 -> 0; matrix products, arithmetic and copies ran while one was open for 8% -> 1% of each run, Pallas kernels for 0% -> 6%
where the time goes in v1:
time: 90.4 us; the launch traced here: 90.1 us
  Pallas kernels  85.9 us (95%)
  starting transfers between devices  3.02 us (3%)
  local copies, waits for them, and re-layouts  1.17 us (1%)
    pallas_call x1, Pallas kernels, combine(): pl.pallas_call(combine_kernel, out_shape=jax.ShapeDtypeStruct((128, 128),...  26.3 us
    pallas_call x1, Pallas kernels, share(): pl.pallas_call(share_kernel, out_shape=jax.ShapeDtypeStruct((4 * RUN * RO...  20.7 us
    pallas_call x1, Pallas kernels, project(): pl.pallas_call(project_kernel, out_shape=(jax.ShapeDtypeStruct((256, 4096...  19.6 us
    pallas_call x2, Pallas kernels, window_sums(): pl.pallas_call(functools.partial(window_kernel, own), out_shape=jax.Shape...  10.3 us
    pallas_call x1, Pallas kernels, body(): pl.pallas_call(filter_kernel, out_shape=jax.ShapeDtypeStruct((1, 4096), F...  9 us
    ppermute x1, starting transfers between devices, body(): lax.ppermute(delay, 'vox', [(i, (i + 1) % SLABS) for i in range(SLABS)])  3.02 us
  transfers between devices with their start and end apart: 1, of which 0 were waited for; matrix products, arithmetic and copies ran while one was open for 1% of the time, Pallas kernels for 6%

profile of v1, /device:TPU:1, one launch (start us, length us, event | category | flops | bytes accessed | tf_op | source)
XLA Modules:
  0.0 90.1 jit_solution(1136810896046516219)
XLA Ops:
  0.0 0.0 copy-start
  0.0 3.0 %collective-permute-start = (s32[1,256]{1,0:T(1,128)}, s32[1,256]{1,0:T(1,128)S(1)}, u32[]{:S(2)}, u32[]{:S(2)}) collective-permute-start(s32[1,256]{1,0:T(1,128)} %bitcast.13), channel_id=1, source_target_pairs={{0,1},{1,2},{2,3},{3,4},{4,5},{5,6},{6,7},{7,8},{8,9},{9,10},{10,1... | collective-permute-start | bytes 3080 | tf_op jit(solution)/shard_map/ppermute | solution.py:425
  3.0 5.2 %window_own.1.own_ref = f32[1024,128]{1,0:T(8,128)} custom-call(s32[64,128]{1,0:T(8,128)} %bitcast.9, s32[1,256]{1,0:T(1,128)} %bitcast.14, bf16[32,8,6400]{2,1,0:T(8,128)(2,1)} %bitcast.7), custom_call_target="tpu_custom_call" | custom-call | flops 100000000 | bytes 4000000 | tf_op jit(solution)/shard_map/window_own/pallas_call | solution.py:93
  8.2 0.0 copy-done
  8.2 0.6 pad.4.prior_ref
  8.8 0.0 collective-permute-done.delay_ref
  8.8 0.0 copy-start.1
  8.8 0.6 copy-done.1
  9.4 5.1 %window_prev.1.prev_ref = bf16[1024,128]{1,0:T(8,128)(2,1)} custom-call(s32[64,128]{1,0:T(8,128)} %bitcast.10, s32[1,256]{1,0:T(1,128)} %copy-done.1, bf16[32,8,6400]{2,1,0:T(8,128)(2,1)} %bitcast.8), custom_call_target="tpu_custom_call" | custom-call | flops 100000000 | bytes 4000000 | tf_op jit(solution)/shard_map/window_prev/pallas_call | solution.py:93
  14.5 20.7 %share.1.all_ref = bf16[4096,128]{1,0:T(8,128)(2,1)} custom-call(f32[1024,128]{1,0:T(8,128)} %window_own.1.own_ref, bf16[1024,128]{1,0:T(8,128)(2,1)} %window_prev.1.prev_ref), custom_call_target="tpu_custom_call" | custom-call | tf_op jit(solution)/shard_map/share/pallas_call | solution.py:150
  35.2 19.6 %project.1 = (bf16[256,4096]{1,0:T(8,128)(2,1)}, f32[256,256]{1,0:T(8,128)}) custom-call(s32[64,128]{1,0:T(8,128)} %bitcast.11, f32[1,128]{1,0:T(1,128)} %bitcast.15, f32[1,128]{1,0:T(1,128)} %bitcast.16, f32[1,128]{1,0:T(1,128)} %bitcast.17, bf16[4096,128]{1,0:T(8,128)(2,1)} %share.1.all_ref), custom_call_target="tpu_custom_call" | custom-call | tf_op jit(solution)/shard_map/project/pallas_call | solution.py:264
  54.8 26.3 %combine.1.gram_ref = f32[128,128]{1,0:T(8,128)} custom-call(f32[256,256]{1,0:T(8,128)} %get-tuple-element.7.wide_ref), custom_call_target="tpu_custom_call" | custom-call | tf_op jit(solution)/shard_map/combine/pallas_call | solution.py:403
  81.1 9.0 %filter.1 = f32[1,4096]{1,0:T(1,128)} custom-call(f32[128,128]{1,0:T(8,128)} %combine.1.gram_ref, f32[32,128]{1,0:T(8,128)} %pad.4.prior_ref, bf16[256,4096]{1,0:T(8,128)(2,1)} %get-tuple-element.8.beam_ref), custom_call_target="tpu_custom_call" | custom-call | tf_op jit(solution)/shard_map/filter/pallas_call | solution.py:439
Async XLA Ops:
  0.0 8.2 %copy-start = (f32[100,30]{0,1:T(8,128)S(1)}, f32[100,30]{0,1:T(8,128)}, u32[]{:S(2)}) copy-start(f32[100,30]{0,1:T(8,128)} %param.13) | copy-start | bytes 36004
  0.0 8.8 %collective-permute-start = (s32[1,256]{1,0:T(1,128)}, s32[1,256]{1,0:T(1,128)S(1)}, u32[]{:S(2)}, u32[]{:S(2)}) collective-permute-start(s32[1,256]{1,0:T(1,128)} %bitcast.13), channel_id=1, source_target_pairs={{0,1},{1,2},{2,3},{3,4},{4,5},{5,6},{6,7},{7,8},{8,9},{9,10},{10,1... | collective-permute-start | bytes 3080 | tf_op jit(solution)/shard_map/ppermute | solution.py:425
  8.8 0.6 copy-start.1

commit v2 on v0

v2 whole, which is shorter than its diff:
```python
import jax
import jax.numpy as jnp
from jax import lax
from jax.experimental import pallas as pl
from jax.experimental.pallas import tpu as pltpu
from jax.sharding import PartitionSpec as P

MESH = pl.DeviceIdType.MESH
FRAMES = 100
RANK = 30
PAIRS = 50
ROWS = 112
RUN = 16
GROUP = 32
SLABS = 64
SIZE = RUN // 2 * ROWS
VOXELS = 4096
VMEM = pltpu.VMEM
F32 = jnp.float32
BF16 = jnp.bfloat16


def iota(shape, dim):
    return lax.broadcasted_iota(jnp.int32, shape, dim)


def run_start(aperture_ref, slab, group):
    start = jnp.int32(0)
    for b in range(GROUP):
        here = aperture_ref[slab, group * GROUP + b]
        before = aperture_ref[slab, group * GROUP + (b - 1) % GROUP]
        start = start + b * here * (1 - before)
    return start


def window_sums(own, start, gates, delay_ref, echo_ref, moved_ref, rows_ref):
    lane = iota((8, 128), 1)
    sub = iota((8, 128), 0)
    sample = lane & 63
    low = jnp.broadcast_to(delay_ref[0:1, 0:128], (8, 128))
    high = jnp.broadcast_to(delay_ref[0:1, 128:256], (8, 128))

    def pair(i, carry):
        blocks, picks, keeps = [], [], []
        for q in range(2):
            block = lax.rem(start + 2 * i + q, GROUP)
            table = jnp.where(jnp.full((8, 128), block, jnp.int32) < 16, low, high)
            delay = jnp.take_along_axis(table, (block & 15) * 8 + sub, axis=1)
            if own:
                picks.append((lane + delay) & 127)
                keeps.append(sample + delay < 64)
            else:
                picks.append((lane + delay + 64) & 127)
                keeps.append(sample + delay >= 64)
            blocks.append(block)
        for t in range(PAIRS):
            parts = []
            for q in range(2):
                values = echo_ref[blocks[q], :, t * 128 : (t + 1) * 128].astype(F32)
                values = jnp.take_along_axis(values, picks[q], axis=1)
                parts.append(jnp.where(keeps[q], values, 0.0))
            moved_ref[pl.ds(pl.multiple_of(i * 16, 16), 16), t * 128 : (t + 1) * 128] = (
                jnp.concatenate(parts, axis=0).astype(BF16)
            )
        return carry

    lax.fori_loop(0, RUN // 2, pair, 0)
    first = iota((8, 128), 1) < 64
    for c in range(PAIRS // 2):
        sums = jnp.dot(
            gates, moved_ref[:, c * 256 : (c + 1) * 256], preferred_element_type=F32
        )
        for q in range(2):
            p = 2 * c + q
            even = sums[0:8, q * 128 : (q + 1) * 128]
            odd = sums[8:16, q * 128 : (q + 1) * 128]
            rows_ref[pl.ds(2 * p, 8, stride=ROWS), :] = jnp.where(
                first, even, pltpu.roll(odd, 64, 1)
            )
            rows_ref[pl.ds(2 * p + 1, 8, stride=ROWS), :] = jnp.where(
                first, pltpu.roll(even, 64, 1), odd
            )


def sweep(gram, rows):
    product = jnp.dot(rows, gram, precision=lax.Precision.HIGHEST, preferred_element_type=F32)
    normal = lax.dot_general(
        product,
        product,
        (((1,), (1,)), ((), ())),
        precision=lax.Precision.HIGHEST,
        preferred_element_type=F32,
    )
    normal = jnp.concatenate([normal, jnp.zeros((32, 96), F32)], axis=1)
    sub = iota((32, 128), 0)
    scale = jnp.zeros((32, 128), F32)
    for j in range(RANK):
        column = jnp.take_along_axis(normal, jnp.full((32, 128), j, jnp.int32), axis=1)
        pivot = jnp.broadcast_to(column[j : j + 1], (32, 128))
        scale = jnp.where(sub == j, lax.rsqrt(pivot), scale)
        factor = jnp.where(sub > j, column / pivot, 0.0)
        normal = normal - factor * normal[j : j + 1]
        product = product - factor * product[j : j + 1]
    return product * scale


def kernel(
    aperture_smem,
    aperture_ref,
    delay_ref,
    offset_ref,
    slope_ref,
    tilt_ref,
    prior_ref,
    echo_hbm,
    out_ref,
    echo_ref,
    moved_ref,
    rows_ref,
    own_ref,
    prev_ref,
    next_ref,
    prev_delay_ref,
    all_ref,
    table_ref,
    point_ref,
    total_ref,
    beam_ref,
    wide_ref,
    mine_ref,
    got_ref,
    sum_ref,
    gram_ref,
    basis_ref,
    echo_sem,
    ring_send,
    ring_recv,
    peer_send,
    peer_recv,
    send,
    recv,
):
    group = lax.axis_index("chan")
    slab = lax.axis_index("vox")
    before = lax.rem(slab + SLABS - 1, SLABS)
    after = lax.rem(slab + 1, SLABS)
    core = lax.rem(slab, 2)
    chip = slab // 2
    y, z = chip // 8, lax.rem(chip, 8)
    me = group * 2 + core
    around = []
    for d in range(1, 8):
        peer = lax.rem(me + d, 8)
        around.append((peer, (peer // 2, slab - core + lax.rem(peer, 2))))
    along_y = [(group, (lax.rem(y + d, 4) * 8 + z) * 2 + core) for d in range(1, 4)]
    along_z = [(group, (y * 8 + lax.rem(z + d, 8)) * 2 + core) for d in range(1, 8)]
    barrier = pltpu.get_barrier_semaphore()
    places = [(group, before), (group, after)] + [a[1] for a in around] + along_y + along_z
    for place in places:
        pl.semaphore_signal(barrier, inc=1, device_id=place, device_id_type=MESH)
    fetch = pltpu.make_async_copy(echo_hbm, echo_ref, echo_sem)
    fetch.start()

    def copy(src, dst, place, sends, recvs, k):
        return pltpu.make_async_remote_copy(
            src_ref=src,
            dst_ref=dst,
            send_sem=sends.at[k],
            recv_sem=recvs.at[k],
            device_id=place,
            device_id_type=MESH,
        )

    lane1 = iota((1, 128), 1)

    def edges(row):
        last = jnp.where(
            lane1 % GROUP == 0, pltpu.roll(row, 97, 1), pltpu.roll(row, 1, 1)
        )
        return (row * (1 - last) * (lane1 % GROUP)).astype(F32)

    row = aperture_ref[pl.ds(slab, 1), :]
    prev_row = aperture_ref[pl.ds(before, 1), :]
    first_of = edges(row)
    order = iota((RUN, 128), 0)
    order = jnp.where(order < 8, 2 * order, 2 * order - 15)
    member = iota((RUN, 128), 1) // 8 == order

    def gates_of(r):
        count = jnp.sum(
            jnp.where(lane1 // GROUP == group, r.astype(F32), 0.0), axis=1, keepdims=True
        )
        return jnp.where(member & (order.astype(F32) < count), 1.0 / 32, 0.0).astype(BF16)

    rows_ref[...] = jnp.zeros_like(rows_ref)
    lane8 = iota((8, 128), 1)
    sub8 = iota((8, 128), 0)
    depth = (lane8 & 63).astype(F32)
    side = (lane8 >> 6).astype(F32)
    level = iota((16, 128), 0)

    def tables(r, begin, end):
        source = lax.rem(group + r, 4)
        start = jnp.sum(
            jnp.where(lane1 // GROUP == source, first_of, 0.0), axis=1, keepdims=True
        ).astype(jnp.int32)
        bases, tilts = [], []
        for s in range(2):
            pick = source * GROUP + ((jnp.broadcast_to(start, (8, 128)) + sub8 + 8 * s) & 31)

            def values(ref):
                return jnp.take_along_axis(
                    jnp.broadcast_to(ref[0:1, :], (8, 128)), pick, axis=1
                )

            bases.append(values(offset_ref) + values(slope_ref) * depth)
            tilts.append(values(tilt_ref))

        def tile(t, carry):
            lateral = side + (64 * group + 2 * t).astype(F32)
            columns = pl.ds(pl.multiple_of(t * 128, 128), 128)
            for s in range(2):
                position = bases[s] + tilts[s] * lateral
                node = jnp.floor(position)
                right = position - node
                point_ref[s * 24 : s * 24 + 8, :] = node
                point_ref[s * 24 + 8 : s * 24 + 16, :] = 1.0 - right
                point_ref[s * 24 + 16 : s * 24 + 24, :] = right
            for s in range(2):
                for b in range(8):
                    node, left, right = [
                        jnp.concatenate([v, v], axis=0).astype(BF16)
                        for v in [
                            jnp.broadcast_to(
                                point_ref[s * 24 + 8 * k + b : s * 24 + 8 * k + b + 1, :],
                                (8, 128),
                            )
                            for k in range(3)
                        ]
                    ]
                    for k in range(4):
                        at = (level + 16 * k).astype(BF16)
                        past = (level + (16 * k - 1)).astype(BF16)
                        weight = jnp.where(
                            at == node,
                            left,
                            jnp.where(past == node, right, jnp.zeros_like(right)),
                        )
                        base = r * 1024 + (s * 8 + b) * 64 + k * 16
                        table_ref[base : base + 16, columns] = weight
            return carry

        lax.fori_loop(begin, end, tile, 0)

    start = run_start(aperture_smem, slab, group)
    prev_start = run_start(aperture_smem, before, group)
    fetch.wait()
    window_sums(True, start, gates_of(row), delay_ref, echo_ref, moved_ref, rows_ref)
    own_ref[...] = rows_ref[...]
    pl.semaphore_wait(barrier, len(places))

    step = copy(delay_ref, prev_delay_ref, (group, after), ring_send, ring_recv, 0)
    step.start()
    tables(0, 0, 32)
    step.wait()
    window_sums(
        False, prev_start, gates_of(prev_row), prev_delay_ref, echo_ref, moved_ref, rows_ref
    )
    prev_ref[...] = rows_ref[...].astype(BF16)
    step = copy(prev_ref, next_ref, (group, before), ring_send, ring_recv, 1)
    step.start()
    tables(1, 0, 32)
    tables(3, 0, 16)
    step.wait()
    live = jnp.where(slab < SLABS - 1, 1.0, 0.0)
    all_ref[0] = (own_ref[...] + next_ref[...].astype(F32) * live).astype(BF16)
    peers = {
        d: copy(
            all_ref.at[0],
            all_ref.at[4 - d],
            (lax.rem(group + d, 4), slab),
            peer_send,
            peer_recv,
            4 - d,
        )
        for d in range(1, 4)
    }
    for d in (1, 3, 2):
        peers[d].start()
    tables(3, 16, 32)
    tables(2, 0, 32)

    def project(sources, first, last):
        def tile(n, carry):
            columns = pl.ds(pl.multiple_of(n * 256, 256), 256)
            total = None if first else total_ref[:, columns]
            for r in sources:
                for c in range(4):
                    left = jnp.concatenate(
                        [
                            all_ref[r, 2 * c * ROWS : (2 * c + 1) * ROWS, :],
                            all_ref[r, (2 * c + 1) * ROWS : (2 * c + 2) * ROWS, :],
                        ],
                        axis=1,
                    )
                    base = r * 1024 + c * 256
                    part = jnp.dot(
                        left, table_ref[base : base + 256, columns], preferred_element_type=F32
                    )
                    total = part if total is None else total + part
            if not last:
                total_ref[:, columns] = total
                return carry
            high = total.astype(BF16)
            low = (total - high.astype(F32)).astype(BF16)
            blank = jnp.zeros((128 - ROWS, 256), BF16)
            both = jnp.concatenate([high, blank, low, blank], axis=0)
            beam_ref[:, columns] = both
            wide_ref[...] += lax.dot_general(
                both, both, (((1,), (1,)), ((), ())), preferred_element_type=F32
            )
            return carry

        lax.fori_loop(0, VOXELS // 256, tile, 0)

    project((0,), True, False)
    peers[1].wait_recv()
    peers[3].wait_recv()
    project((1, 3), False, False)
    wide_ref[...] = jnp.zeros_like(wide_ref)
    peers[2].wait_recv()
    project((2,), False, True)
    for d in range(1, 4):
        peers[d].wait_send()

    mine_ref[...] = (
        wide_ref[0:128, 0:128]
        + wide_ref[128:256, 0:128]
        + wide_ref[0:128, 128:256]
        + wide_ref[128:256, 128:256]
    )

    def rows(k):
        return pl.ds(pl.multiple_of(k * 16, 16), 16)

    def exchange(copies):
        for c in copies:
            c.start()
        for c in copies:
            c.wait()

    exchange(
        [
            copy(mine_ref.at[rows(peer)], got_ref.at[k], place, send, recv, k)
            for k, (peer, place) in enumerate(around)
        ]
    )
    total = mine_ref[rows(me), :]
    for k in range(7):
        total = total + got_ref[k]
    sum_ref[0] = total
    exchange(
        [
            copy(sum_ref.at[0], got_ref.at[7 + k], place, send, recv, 7 + k)
            for k, place in enumerate(along_y)
        ]
    )
    for k in range(3):
        total = total + got_ref[7 + k]
    sum_ref[1] = total
    exchange(
        [
            copy(sum_ref.at[1], got_ref.at[10 + k], place, send, recv, 10 + k)
            for k, place in enumerate(along_z)
        ]
    )
    for k in range(7):
        total = total + got_ref[10 + k]
    gram_ref[rows(me), :] = total
    exchange(
        [
            copy(gram_ref.at[rows(me)], gram_ref.at[rows(me)], place, send, recv, 17 + k)
            for k, (_, place) in enumerate(around)
        ]
    )

    gram = gram_ref[...]
    basis_ref[...] = jnp.zeros_like(basis_ref)
    basis_ref[0:RANK, 0:FRAMES] = prior_ref[...]
    basis = sweep(gram, basis_ref[...])
    basis = sweep(gram, basis)
    overlap = lax.dot_general(
        basis,
        basis,
        (((0,), (0,)), ((), ())),
        precision=lax.Precision.HIGHEST,
        preferred_element_type=F32,
    )
    keep = jnp.where(iota((128, 128), 0) == iota((128, 128), 1), 1.0, 0.0) - overlap
    high = keep.astype(BF16)
    low = (keep - high.astype(F32)).astype(BF16)
    twice = jnp.concatenate([high, high], axis=1)
    for c in range(VOXELS // 256):
        beam = beam_ref[:, c * 256 : (c + 1) * 256]
        clean = jnp.dot(twice, beam, preferred_element_type=F32)
        clean = clean + jnp.dot(low, beam[0:128], preferred_element_type=F32)
        out_ref[:, c * 256 : (c + 1) * 256] = jnp.sum(
            clean * clean, axis=0, keepdims=True
        ) * (1.0 / FRAMES)


def body(echo_data, delays, aperture, offset, depth_slope, lateral_tilt, prior_basis):
    vmem = pl.BlockSpec(memory_space=VMEM)
    smem = pl.BlockSpec(memory_space=pltpu.SMEM)
    dma = pltpu.SemaphoreType.DMA
    return pl.pallas_call(
        kernel,
        out_shape=jax.ShapeDtypeStruct((1, VOXELS), F32),
        in_specs=[smem] + [vmem] * 6 + [pl.BlockSpec(memory_space=pl.ANY)],
        out_specs=vmem,
        scratch_shapes=[
            VMEM((GROUP, 8, 128 * PAIRS), BF16),
            VMEM((128, 128 * PAIRS), BF16),
            VMEM((SIZE, 128), F32),
            VMEM((SIZE, 128), F32),
            VMEM((SIZE, 128), BF16),
            VMEM((SIZE, 128), BF16),
            VMEM((1, 256), jnp.int32),
            VMEM((4, SIZE, 128), BF16),
            VMEM((4 * RUN * 64, VOXELS), BF16),
            VMEM((48, 128), F32),
            VMEM((ROWS, VOXELS), F32),
            VMEM((256, VOXELS), BF16),
            VMEM((256, 256), F32),
            VMEM((128, 128), F32),
            VMEM((17, 16, 128), F32),
            VMEM((2, 16, 128), F32),
            VMEM((128, 128), F32),
            VMEM((32, 128), F32),
            dma,
            dma((2,)),
            dma((2,)),
            dma((4,)),
            dma((4,)),
            dma((24,)),
            dma((24,)),
        ],
        compiler_params=pltpu.CompilerParams(
            collective_id=0, has_side_effects=True, vmem_limit_bytes=62 * 1024 * 1024
        ),
        name="doppler",
    )(
        aperture.T,
        aperture.T,
        delays.reshape(1, 256),
        offset.reshape(1, 128),
        depth_slope.reshape(1, 128),
        lateral_tilt.reshape(1, 128),
        prior_basis.T,
        echo_data.reshape(GROUP, 8, 128 * PAIRS),
    )


def solution(mesh):
    in_specs = (
        P("chan", "vox", None),
        P("chan", "vox"),
        P(),
        P(None, "vox"),
        P(None, "vox"),
        P(None, "vox"),
        P(),
    )
    out_specs = P("vox", "chan")
    return jax.shard_map(body, mesh=mesh, in_specs=in_specs, out_specs=out_specs, check_vma=False)
```

time: 317 us -> 70.4 us (0.22)
  blocking collectives: 76.4 us -> 0 us
  matrix products: 68.8 us -> 0 us
  Pallas kernels: 0 us -> 68.8 us
  waiting for transfers between devices: 58.1 us -> 0 us
  local copies, waits for them, and re-layouts: 57 us -> 1.32 us
  other arithmetic: 36.3 us -> 0 us
  between operations: 13.6 us -> 0.01 us
  starting transfers between devices: 5.23 us -> 0 us
    psum x1 -> x0, blocking collectives: 76.4 us -> none  [body(): gram_matrix = lax.psum(local_gram, ('chan', 'vox'))]
    pallas_call x0 -> x1, Pallas kernels: none -> 68.8 us  [body(): pl.pallas_call(kernel, out_shape=jax.ShapeDtypeStruct((1, VOXELS), F32),...]
    dot_general x15 -> x0, matrix products: 68.3 us -> none  [the longest x8 61.4 us: one_turn(): jnp.einsum('bfk,bkv->fv', pieces[0], table, preferred_element_type=jnp.fl...]
    reduce_scatter x1 -> x0, waiting for transfers between devices: 45.8 us -> none  [body(): lax.psum_scatter(partial_value.astype(jnp.bfloat16), 'chan', scatter_dime...]
    another operation x6 -> x0, local copies, waits for them, and re-layouts: 19.6 us -> none  [the longest x2 19.3 us: body(): lower_part = echo_rows.reshape(kept, BLOCK_CH, frames, WINDOW)]
    gather x2 -> x0, local copies, waits for them, and re-layouts: 18.6 us -> none  [take_window(): lax.dynamic_slice(row, (jnp.zeros((), jnp.int32), start), (row.shape[0],...]
    reshape x6 -> x0, local copies, waits for them, and re-layouts: 17.3 us -> none  [the longest x2 17 us: body(): upper_part = upper_rows.reshape(kept, BLOCK_CH, frames, WINDOW)]
    another operation x10 -> x0, other arithmetic: 12.7 us -> none  [the longest x6 6.84 us: refine_basis(): factor = jnp.linalg.cholesky(normal_matrix)]
  transfers between devices with their start and end apart: 2 -> 0, of which waited for: 2 -> 0; matrix products, arithmetic and copies ran while one was open for 8% -> 0% of each run, Pallas kernels for 0% -> 0%
where the time goes in v2:
time: 70.4 us; the launch traced here: 70.1 us
  Pallas kernels  68.8 us (98%)
  local copies, waits for them, and re-layouts  1.32 us (2%)
    pallas_call x1, Pallas kernels, body(): pl.pallas_call(kernel, out_shape=jax.ShapeDtypeStruct((1, VOXELS), F32),...  68.8 us

profile of v2, /device:TPU:1, one launch (start us, length us, event | category | flops | bytes accessed | tf_op | source)
XLA Modules:
  0.0 70.1 jit_solution(7909026311202504982)
XLA Ops:
  0.0 68.8 %doppler.1 = f32[1,4096]{1,0:T(1,128)} custom-call(s32[64,128]{1,0:T(8,128)} %bitcast.8, s32[64,128]{1,0:T(8,128)} %bitcast.9, s32[1,256]{1,0:T(1,128)} %bitcast.11, f32[1,128]{1,0:T(1,128)} %bitcast.12, f32[1,128]{1,0:T(1,128)} %bitcast.13, f32[1,128]{1,0:T(1,128)} %bitcast.14, f32[30,100]{1,0:T(8,128)} %bitcast.10, bf16[32,8,6400]{2,1,0:T(8,128)(2,1)} %bitcast.7), custom_call_target="tpu_custom_call" | custom-call | tf_op jit(solution)/shard_map/doppler/pallas_call | solution.py:416
  68.8 1.3 %copy.9 = f32[1,4096]{1,0:T(1,128)} copy(f32[1,4096]{1,0:T(1,128)} %doppler.1) | data formatting | bytes 32768

commit v3 on v2

--- a/solution.py
+++ b/solution.py
@@ -9,7 +9,9 @@
 FRAMES = 100
 RANK = 30
 PAIRS = 50
-ROWS = 112
+ROWS = 104
+HALF = 4 * ROWS
+STEP = 15
 RUN = 16
 GROUP = 32
 SLABS = 64
@@ -40,10 +42,10 @@
     low = jnp.broadcast_to(delay_ref[0:1, 0:128], (8, 128))
     high = jnp.broadcast_to(delay_ref[0:1, 128:256], (8, 128))
 
-    def pair(i, carry):
-        blocks, picks, keeps = [], [], []
-        for q in range(2):
-            block = lax.rem(start + 2 * i + q, GROUP)
+    def blocks(i, carry):
+        places, picks, keeps = [], [], []
+        for q in range(4):
+            block = lax.rem(start + 4 * i + q, GROUP)
             table = jnp.where(jnp.full((8, 128), block, jnp.int32) < 16, low, high)
             delay = jnp.take_along_axis(table, (block & 15) * 8 + sub, axis=1)
             if own:
@@ -52,24 +54,23 @@
             else:
                 picks.append((lane + delay + 64) & 127)
                 keeps.append(sample + delay >= 64)
-            blocks.append(block)
+            places.append(block)
         for t in range(PAIRS):
             parts = []
-            for q in range(2):
-                values = echo_ref[blocks[q], :, t * 128 : (t + 1) * 128].astype(F32)
+            for q in range(4):
+                values = echo_ref[places[q], :, t * 128 : (t + 1) * 128].astype(F32)
                 values = jnp.take_along_axis(values, picks[q], axis=1)
                 parts.append(jnp.where(keeps[q], values, 0.0))
-            moved_ref[pl.ds(pl.multiple_of(i * 16, 16), 16), t * 128 : (t + 1) * 128] = (
-                jnp.concatenate(parts, axis=0).astype(BF16)
-            )
+            moved_ref[t, pl.ds(pl.multiple_of(i * 32, 32), 32), :] = jnp.concatenate(
+                parts, axis=0
+            ).astype(BF16)
         return carry
 
-    lax.fori_loop(0, RUN // 2, pair, 0)
+    lax.fori_loop(0, RUN // 4, blocks, 0)
     first = iota((8, 128), 1) < 64
     for c in range(PAIRS // 2):
-        sums = jnp.dot(
-            gates, moved_ref[:, c * 256 : (c + 1) * 256], preferred_element_type=F32
-        )
+        both = jnp.concatenate([moved_ref[2 * c], moved_ref[2 * c + 1]], axis=1)
+        sums = jnp.dot(gates, both, preferred_element_type=F32)
         for q in range(2):
             p = 2 * c + q
             even = sums[0:8, q * 128 : (q + 1) * 128]
@@ -94,13 +95,20 @@
     normal = jnp.concatenate([normal, jnp.zeros((32, 96), F32)], axis=1)
     sub = iota((32, 128), 0)
     scale = jnp.zeros((32, 128), F32)
-    for j in range(RANK):
-        column = jnp.take_along_axis(normal, jnp.full((32, 128), j, jnp.int32), axis=1)
-        pivot = jnp.broadcast_to(column[j : j + 1], (32, 128))
-        scale = jnp.where(sub == j, lax.rsqrt(pivot), scale)
-        factor = jnp.where(sub > j, column / pivot, 0.0)
-        normal = normal - factor * normal[j : j + 1]
-        product = product - factor * product[j : j + 1]
+    for begin in range(0, RANK, STEP):
+        columns = [
+            jnp.take_along_axis(normal, jnp.full((32, 128), begin + i, jnp.int32), axis=1)
+            for i in range(STEP)
+        ]
+        for i in range(STEP):
+            j = begin + i
+            pivot = jnp.broadcast_to(columns[i][j : j + 1], (32, 128))
+            factor = jnp.where(sub > j, columns[i] / pivot, 0.0)
+            scale = jnp.where(sub == j, lax.rsqrt(pivot), scale)
+            for k in range(i + 1, STEP):
+                columns[k] = columns[k] - factor * columns[k][j : j + 1]
+            normal = normal - factor * normal[j : j + 1]
+            product = product - factor * product[j : j + 1]
     return product * scale
 
 
@@ -122,7 +130,7 @@
     next_ref,
     prev_delay_ref,
     all_ref,
-    table_ref,
+    place_ref,
     point_ref,
     total_ref,
     beam_ref,
@@ -198,13 +206,14 @@
     depth = (lane8 & 63).astype(F32)
     side = (lane8 >> 6).astype(F32)
     level = iota((16, 128), 0)
-
-    def tables(r, begin, end):
+    levels = [(level + 16 * k).astype(BF16) for k in range(4)]
+    pasts = [(level + (16 * k - 1)).astype(BF16) for k in range(4)]
+
+    def place_blocks(r):
         source = lax.rem(group + r, 4)
         start = jnp.sum(
             jnp.where(lane1 // GROUP == source, first_of, 0.0), axis=1, keepdims=True
         ).astype(jnp.int32)
-        bases, tilts = [], []
         for s in range(2):
             pick = source * GROUP + ((jnp.broadcast_to(start, (8, 128)) + sub8 + 8 * s) & 31)
 
@@ -213,55 +222,19 @@
                     jnp.broadcast_to(ref[0:1, :], (8, 128)), pick, axis=1
                 )
 
-            bases.append(values(offset_ref) + values(slope_ref) * depth)
-            tilts.append(values(tilt_ref))
-
-        def tile(t, carry):
-            lateral = side + (64 * group + 2 * t).astype(F32)
-            columns = pl.ds(pl.multiple_of(t * 128, 128), 128)
-            for s in range(2):
-                position = bases[s] + tilts[s] * lateral
-                node = jnp.floor(position)
-                right = position - node
-                point_ref[s * 24 : s * 24 + 8, :] = node
-                point_ref[s * 24 + 8 : s * 24 + 16, :] = 1.0 - right
-                point_ref[s * 24 + 16 : s * 24 + 24, :] = right
-            for s in range(2):
-                for b in range(8):
-                    node, left, right = [
-                        jnp.concatenate([v, v], axis=0).astype(BF16)
-                        for v in [
-                            jnp.broadcast_to(
-                                point_ref[s * 24 + 8 * k + b : s * 24 + 8 * k + b + 1, :],
-                                (8, 128),
-                            )
-                            for k in range(3)
-                        ]
-                    ]
-                    for k in range(4):
-                        at = (level + 16 * k).astype(BF16)
-                        past = (level + (16 * k - 1)).astype(BF16)
-                        weight = jnp.where(
-                            at == node,
-                            left,
-                            jnp.where(past == node, right, jnp.zeros_like(right)),
-                        )
-                        base = r * 1024 + (s * 8 + b) * 64 + k * 16
-                        table_ref[base : base + 16, columns] = weight
-            return carry
-
-        lax.fori_loop(begin, end, tile, 0)
-
+            tilt = values(tilt_ref)
+            lateral = side + (64 * group).astype(F32)
+            place_ref[r, s, 0] = values(offset_ref) + values(slope_ref) * depth + tilt * lateral
+            place_ref[r, s, 1] = tilt
+
+    pl.semaphore_wait(barrier, len(places))
+    step = copy(delay_ref, prev_delay_ref, (group, after), ring_send, ring_recv, 0)
+    step.start()
     start = run_start(aperture_smem, slab, group)
     prev_start = run_start(aperture_smem, before, group)
     fetch.wait()
     window_sums(True, start, gates_of(row), delay_ref, echo_ref, moved_ref, rows_ref)
     own_ref[...] = rows_ref[...]
-    pl.semaphore_wait(barrier, len(places))
-
-    step = copy(delay_ref, prev_delay_ref, (group, after), ring_send, ring_recv, 0)
-    step.start()
-    tables(0, 0, 32)
     step.wait()
     window_sums(
         False, prev_start, gates_of(prev_row), prev_delay_ref, echo_ref, moved_ref, rows_ref
@@ -269,76 +242,130 @@
     prev_ref[...] = rows_ref[...].astype(BF16)
     step = copy(prev_ref, next_ref, (group, before), ring_send, ring_recv, 1)
     step.start()
-    tables(1, 0, 32)
-    tables(3, 0, 16)
+    for r in range(4):
+        place_blocks(r)
+    blank = jnp.zeros((128 - ROWS, 128), BF16)
+    for t in range(VOXELS // 128):
+        beam_ref[t, ROWS:128, :] = blank
+        beam_ref[t, 128 + ROWS : 256, :] = blank
+    live = jnp.where(slab < SLABS - 1, 1.0, 0.0)
     step.wait()
-    live = jnp.where(slab < SLABS - 1, 1.0, 0.0)
     all_ref[0] = (own_ref[...] + next_ref[...].astype(F32) * live).astype(BF16)
-    peers = {
-        d: copy(
-            all_ref.at[0],
-            all_ref.at[4 - d],
-            (lax.rem(group + d, 4), slab),
-            peer_send,
-            peer_recv,
-            4 - d,
+    right, left = (lax.rem(group + 1, 4), slab), (lax.rem(group + 3, 4), slab)
+    upper, lower = pl.ds(0, HALF), pl.ds(HALF, HALF)
+
+    def pass_on(source, target, part, place, k):
+        return copy(
+            all_ref.at[source, part], all_ref.at[target, part], place, peer_send, peer_recv, k
         )
-        for d in range(1, 4)
-    }
-    for d in (1, 3, 2):
-        peers[d].start()
-    tables(3, 16, 32)
-    tables(2, 0, 32)
-
-    def project(sources, first, last):
-        def tile(n, carry):
-            columns = pl.ds(pl.multiple_of(n * 256, 256), 256)
-            total = None if first else total_ref[:, columns]
-            for r in sources:
-                for c in range(4):
-                    left = jnp.concatenate(
-                        [
-                            all_ref[r, 2 * c * ROWS : (2 * c + 1) * ROWS, :],
-                            all_ref[r, (2 * c + 1) * ROWS : (2 * c + 2) * ROWS, :],
-                        ],
-                        axis=1,
-                    )
-                    base = r * 1024 + c * 256
-                    part = jnp.dot(
-                        left, table_ref[base : base + 256, columns], preferred_element_type=F32
-                    )
-                    total = part if total is None else total + part
-            if not last:
-                total_ref[:, columns] = total
-                return carry
-            high = total.astype(BF16)
-            low = (total - high.astype(F32)).astype(BF16)
-            blank = jnp.zeros((128 - ROWS, 256), BF16)
-            both = jnp.concatenate([high, blank, low, blank], axis=0)
-            beam_ref[:, columns] = both
-            wide_ref[...] += lax.dot_general(
-                both, both, (((1,), (1,)), ((), ())), preferred_element_type=F32
+
+    own_copies = [
+        pass_on(0, 3, upper, right, 0),
+        pass_on(0, 1, lower, left, 1),
+        pass_on(0, 3, lower, right, 2),
+        pass_on(0, 1, upper, left, 3),
+    ]
+    far_copies = [pass_on(3, 2, upper, right, 4), pass_on(1, 2, lower, left, 5)]
+    for c in own_copies:
+        c.start()
+    def weights_of(at, b):
+        node, left, right = [
+            jnp.broadcast_to(point_ref[at + 8 * k + b : at + 8 * k + b + 1, :], (16, 128)).astype(
+                BF16
             )
+            for k in range(3)
+        ]
+        return jnp.concatenate(
+            [
+                jnp.where(
+                    levels[k] == node,
+                    left,
+                    jnp.where(pasts[k] == node, right, jnp.zeros_like(right)),
+                )
+                for k in range(4)
+            ],
+            axis=0,
+        )
+
+    def project(units, first, last):
+        def tile(i, carry):
+            at = 0
+            for v in range(2):
+                for r, s in units:
+                    base, tilt = place_ref[r, s, 0], place_ref[r, s, 1]
+                    for u in range(2):
+                        position = base + tilt * (8 * i + 4 * v + 2 * u).astype(F32)
+                        node = jnp.floor(position)
+                        right = position - node
+                        point_ref[at : at + 8, :] = node
+                        point_ref[at + 8 : at + 16, :] = 1.0 - right
+                        point_ref[at + 16 : at + 24, :] = right
+                        at += 24
+            at = 0
+            for v in range(2):
+                n = 2 * i + v
+                columns = pl.ds(pl.multiple_of(n * 256, 256), 256)
+                total = None if first else total_ref[:, columns]
+                for r, s in units:
+                    for c in range(2):
+                        weights = jnp.concatenate(
+                            [
+                                jnp.concatenate(
+                                    [weights_of(at, b), weights_of(at + 24, b)], axis=1
+                                )
+                                for b in range(4 * c, 4 * c + 4)
+                            ],
+                            axis=0,
+                        )
+                        m = 4 * s + 2 * c
+                        blocks = jnp.concatenate(
+                            [
+                                all_ref[r, m * ROWS : (m + 1) * ROWS, :],
+                                all_ref[r, (m + 1) * ROWS : (m + 2) * ROWS, :],
+                            ],
+                            axis=1,
+                        )
+                        part = jnp.dot(blocks, weights, preferred_element_type=F32)
+                        total = part if total is None else total + part
+                    at += 48
+                if not last:
+                    total_ref[:, columns] = total
+                    continue
+                high = total.astype(BF16)
+                low = (total - high.astype(F32)).astype(BF16)
+                for q in range(2):
+                    lanes = slice(q * 128, q * 128 + 128)
+                    beam_ref[2 * n + q, 0:ROWS, :] = high[:, lanes]
+                    beam_ref[2 * n + q, 128 : 128 + ROWS, :] = low[:, lanes]
             return carry
 
-        lax.fori_loop(0, VOXELS // 256, tile, 0)
-
-    project((0,), True, False)
-    peers[1].wait_recv()
-    peers[3].wait_recv()
-    project((1, 3), False, False)
+        lax.fori_loop(0, VOXELS // 512, tile, 0)
+
+    project(((0, 0), (0, 1)), True, False)
+    for k in range(2):
+        own_copies[k].wait_recv()
+        far_copies[k].start()
+    project(((3, 0), (1, 1)), False, False)
+    for k in range(2, 4):
+        own_copies[k].wait_recv()
+    project(((3, 1), (1, 0)), False, False)
+    for c in far_copies:
+        c.wait_recv()
+    project(((2, 0), (2, 1)), False, True)
+    for c in own_copies + far_copies:
+        c.wait_send()
     wide_ref[...] = jnp.zeros_like(wide_ref)
-    peers[2].wait_recv()
-    project((2,), False, True)
-    for d in range(1, 4):
-        peers[d].wait_send()
-
-    mine_ref[...] = (
-        wide_ref[0:128, 0:128]
-        + wide_ref[128:256, 0:128]
-        + wide_ref[0:128, 128:256]
-        + wide_ref[128:256, 128:256]
-    )
+
+    def square(i, carry):
+        part = jnp.concatenate([beam_ref[8 * i + k] for k in range(8)], axis=1)
+        wide_ref[...] += lax.dot_general(
+            part, part[0:128], (((1,), (1,)), ((), ())), preferred_element_type=F32
+        )
+        return carry
+
+    lax.fori_loop(0, 4, square, 0)
+    cross = wide_ref[128:256, :]
+    mine_ref[...] = wide_ref[0:128, :] + cross + cross.T
 
     def rows(k):
         return pl.ds(pl.multiple_of(k * 16, 16), 16)
@@ -401,37 +428,35 @@
     low = (keep - high.astype(F32)).astype(BF16)
     twice = jnp.concatenate([high, high], axis=1)
     for c in range(VOXELS // 256):
-        beam = beam_ref[:, c * 256 : (c + 1) * 256]
+        beam = jnp.concatenate([beam_ref[2 * c], beam_ref[2 * c + 1]], axis=1)
         clean = jnp.dot(twice, beam, preferred_element_type=F32)
         clean = clean + jnp.dot(low, beam[0:128], preferred_element_type=F32)
-        out_ref[:, c * 256 : (c + 1) * 256] = jnp.sum(
-            clean * clean, axis=0, keepdims=True
-        ) * (1.0 / FRAMES)
+        out_ref[:, c * 256 : (c + 1) * 256] = jnp.sum(clean * clean, axis=0, keepdims=True)
 
 
 def body(echo_data, delays, aperture, offset, depth_slope, lateral_tilt, prior_basis):
     vmem = pl.BlockSpec(memory_space=VMEM)
     smem = pl.BlockSpec(memory_space=pltpu.SMEM)
     dma = pltpu.SemaphoreType.DMA
-    return pl.pallas_call(
+    squares = pl.pallas_call(
         kernel,
         out_shape=jax.ShapeDtypeStruct((1, VOXELS), F32),
         in_specs=[smem] + [vmem] * 6 + [pl.BlockSpec(memory_space=pl.ANY)],
         out_specs=vmem,
         scratch_shapes=[
             VMEM((GROUP, 8, 128 * PAIRS), BF16),
-            VMEM((128, 128 * PAIRS), BF16),
+            VMEM((PAIRS, 128, 128), BF16),
             VMEM((SIZE, 128), F32),
             VMEM((SIZE, 128), F32),
             VMEM((SIZE, 128), BF16),
             VMEM((SIZE, 128), BF16),
             VMEM((1, 256), jnp.int32),
             VMEM((4, SIZE, 128), BF16),
-            VMEM((4 * RUN * 64, VOXELS), BF16),
-            VMEM((48, 128), F32),
+            VMEM((4, 2, 2, 8, 128), F32),
+            VMEM((192, 128), F32),
             VMEM((ROWS, VOXELS), F32),
-            VMEM((256, VOXELS), BF16),
-            VMEM((256, 256), F32),
+            VMEM((VOXELS // 128, 256, 128), BF16),
+            VMEM((256, 128), F32),
             VMEM((128, 128), F32),
             VMEM((17, 16, 128), F32),
             VMEM((2, 16, 128), F32),
@@ -440,8 +465,8 @@
             dma,
             dma((2,)),
             dma((2,)),
-            dma((4,)),
-            dma((4,)),
+            dma((6,)),
+            dma((6,)),
             dma((24,)),
             dma((24,)),
         ],
@@ -459,6 +484,7 @@
         prior_basis.T,
         echo_data.reshape(GROUP, 8, 128 * PAIRS),
     )
+    return squares / FRAMES
 
 
 def solution(mesh):

time: 70.4 us -> 57 us (0.81)
  Pallas kernels: 68.8 us -> 55.4 us
  other arithmetic: 0 us -> 1.34 us
  local copies, waits for them, and re-layouts: 1.32 us -> 0 us
    pallas_call x1, Pallas kernels: 68.8 us -> 55.4 us  [body(): pl.pallas_call(kernel, out_shape=jax.ShapeDtypeStruct((1, VOXELS), F32),...]
    div x0 -> x1, other arithmetic: none -> 1.34 us  [body(): return squares / FRAMES]
    unnamed x1 -> x0, local copies, waits for them, and re-layouts: 1.32 us -> none
where the time goes in v3:
time: 57 us; the launch traced here: 56.8 us
  Pallas kernels  55.4 us (97%)
  other arithmetic  1.34 us (2%)
    pallas_call x1, Pallas kernels, body(): pl.pallas_call(kernel, out_shape=jax.ShapeDtypeStruct((1, VOXELS), F32),...  55.4 us
    div x1, other arithmetic, body(): return squares / FRAMES  1.34 us

profile of v3, /device:TPU:1, one launch (start us, length us, event | category | flops | bytes accessed | tf_op | source)
XLA Modules:
  0.0 56.8 jit_solution(17752235464000761551)
XLA Ops:
  0.0 55.4 %doppler.1 = f32[1,4096]{1,0:T(1,128)} custom-call(s32[64,128]{1,0:T(8,128)} %bitcast.8, s32[64,128]{1,0:T(8,128)} %bitcast.9, s32[1,256]{1,0:T(1,128)} %bitcast.11, f32[1,128]{1,0:T(1,128)} %bitcast.12, f32[1,128]{1,0:T(1,128)} %bitcast.13, f32[1,128]{1,0:T(1,128)} %bitcast.14, f32[30,100]{1,0:T(8,128)} %bitcast.10, bf16[32,8,6400]{2,1,0:T(8,128)(2,1)} %bitcast.7), custom_call_target="tpu_custom_call" | custom-call | tf_op jit(solution)/shard_map/doppler/pallas_call | solution.py:441
  55.4 1.3 %broadcast_multiply_fusion = f32[1,4096]{1,0:T(1,128)} fusion(f32[1,4096]{1,0:T(1,128)} %doppler.1), kind=kLoop, calls=%fused_computation | loop fusion | flops 4096 | bytes 32768 | tf_op jit(solution)/shard_map/div | solution.py:487

commit v4 on v3

v4 whole, which is shorter than its diff:
```python
import jax
import jax.numpy as jnp
from jax import lax
from jax.experimental import pallas as pl
from jax.experimental.pallas import tpu as pltpu
from jax.sharding import PartitionSpec as P

MESH = pl.DeviceIdType.MESH
FRAMES = 100
RANK = 30
PAIRS = 50
ROWS = 104
HALF = 4 * ROWS
SIDE = ROWS // 2
STEP = 15
RUN = 16
GROUP = 32
SLABS = 64
SIZE = RUN // 2 * ROWS
VOXELS = 4096
VMEM = pltpu.VMEM
F32 = jnp.float32
BF16 = jnp.bfloat16


def iota(shape, dim):
    return lax.broadcasted_iota(jnp.int32, shape, dim)


def run_start(run_ref, which, group):
    start = jnp.int32(0)
    before = run_ref[which, group * GROUP + GROUP - 1]
    for b in range(GROUP):
        here = run_ref[which, group * GROUP + b]
        start = start + b * here * (1 - before)
        before = here
    return start


def window_sums(own, half, start, gates, delay_ref, echo_ref, moved_ref, rows_ref):
    lane = iota((8, 128), 1)
    sub = iota((8, 128), 0)
    sample = lane & 63
    low = jnp.broadcast_to(delay_ref[0:1, 0:128], (8, 128))
    high = jnp.broadcast_to(delay_ref[0:1, 128:256], (8, 128))

    def blocks(i, carry):
        places, picks, keeps = [], [], []
        for q in range(4):
            block = lax.rem(start + 8 * half + 4 * i + q, GROUP)
            table = jnp.where(jnp.full((8, 128), block, jnp.int32) < 16, low, high)
            delay = jnp.take_along_axis(table, (block & 15) * 8 + sub, axis=1)
            if own:
                picks.append((lane + delay) & 127)
                keeps.append(sample + delay < 64)
            else:
                picks.append((lane + delay + 64) & 127)
                keeps.append(sample + delay >= 64)
            places.append(block)
        for t in range(PAIRS):
            parts = []
            for q in range(4):
                values = echo_ref[places[q], :, t * 128 : (t + 1) * 128].astype(F32)
                values = jnp.take_along_axis(values, picks[q], axis=1)
                parts.append(jnp.where(keeps[q], values, 0.0))
            moved_ref[t, pl.ds(pl.multiple_of(i * 32, 32), 32), :] = jnp.concatenate(
                parts, axis=0
            ).astype(BF16)
        return carry

    lax.fori_loop(0, RUN // 8, blocks, 0)
    first = lane < 64
    even_frame = (sub & 1) == 0
    for c in range(PAIRS // 2):
        both = jnp.concatenate([moved_ref[2 * c], moved_ref[2 * c + 1]], axis=1)
        sums = jnp.dot(gates, both, preferred_element_type=F32)
        for q in range(2):
            even = sums[0:8, q * 128 : (q + 1) * 128]
            odd = sums[8:16, q * 128 : (q + 1) * 128]
            rows_ref[pl.ds(2 * c + q, 8, stride=SIDE), :] = jnp.where(
                first,
                jnp.where(even_frame, even, pltpu.roll(even, 64, 1)),
                jnp.where(even_frame, pltpu.roll(odd, 64, 1), odd),
            )


def sweep(gram, rows):
    product = jnp.dot(rows, gram, precision=lax.Precision.HIGHEST, preferred_element_type=F32)
    normal = lax.dot_general(
        product,
        product,
        (((1,), (1,)), ((), ())),
        precision=lax.Precision.HIGHEST,
        preferred_element_type=F32,
    )
    normal = jnp.concatenate([normal, jnp.zeros((32, 96), F32)], axis=1)
    sub = iota((32, 128), 0)
    scale = jnp.zeros((32, 128), F32)
    for begin in range(0, RANK, STEP):
        columns = [
            jnp.take_along_axis(normal, jnp.full((32, 128), begin + i, jnp.int32), axis=1)
            for i in range(STEP)
        ]
        for i in range(STEP):
            j = begin + i
            pivot = jnp.broadcast_to(columns[i][j : j + 1], (32, 128))
            factor = jnp.where(sub > j, columns[i] / pivot, 0.0)
            scale = jnp.where(sub == j, lax.rsqrt(pivot), scale)
            for k in range(i + 1, STEP):
                columns[k] = columns[k] - factor * columns[k][j : j + 1]
            normal = normal - factor * normal[j : j + 1]
            product = product - factor * product[j : j + 1]
    return product * scale


def kernel(
    aperture_hbm,
    delay_hbm,
    offset_hbm,
    slope_hbm,
    tilt_hbm,
    prior_hbm,
    echo_hbm,
    out_ref,
    run_ref,
    aperture_ref,
    delay_ref,
    offset_ref,
    slope_ref,
    tilt_ref,
    prior_ref,
    echo_ref,
    moved_ref,
    rows_ref,
    own_ref,
    prev_ref,
    next_ref,
    prev_delay_ref,
    all_ref,
    place_ref,
    point_ref,
    total_ref,
    beam_ref,
    wide_ref,
    mine_ref,
    got_ref,
    sum_ref,
    gram_ref,
    basis_ref,
    power_ref,
    input_sem,
    ring_send,
    ring_recv,
    peer_send,
    peer_recv,
    send,
    recv,
):
    group = lax.axis_index("chan")
    slab = lax.axis_index("vox")
    before = lax.rem(slab + SLABS - 1, SLABS)
    after = lax.rem(slab + 1, SLABS)
    core = lax.rem(slab, 2)
    chip = slab // 2
    y, z = chip // 8, lax.rem(chip, 8)
    me = y * 8 + group * 2 + core
    around = []
    for dy in range(4):
        row_y = lax.rem(y + dy, 4)
        for d in range(8):
            if dy == 0 and d == 0:
                continue
            inner = lax.rem(group * 2 + core + d, 8)
            around.append(
                (row_y * 8 + inner, (inner // 2, (row_y * 8 + z) * 2 + lax.rem(inner, 2)))
            )
    along_z = [(group, (y * 8 + lax.rem(z + d, 8)) * 2 + core) for d in range(1, 8)]
    inputs = [
        pltpu.make_async_copy(source, target, input_sem.at[k])
        for k, (source, target) in enumerate(
            [
                (aperture_hbm.at[pl.ds(slab, 1), :], run_ref.at[pl.ds(0, 1), :]),
                (aperture_hbm.at[pl.ds(before, 1), :], run_ref.at[pl.ds(1, 1), :]),
                (delay_hbm, delay_ref),
                (aperture_hbm, aperture_ref),
                (offset_hbm, offset_ref),
                (slope_hbm, slope_ref),
                (tilt_hbm, tilt_ref),
                (prior_hbm, prior_ref),
                (echo_hbm, echo_ref),
            ]
        )
    ]
    for c in inputs:
        c.start()
    barrier = pltpu.get_barrier_semaphore()
    places = along_z + [a[1] for a in around[::-1]] + [(group, before), (group, after)]
    for place in places:
        pl.semaphore_signal(barrier, inc=1, device_id=place, device_id_type=MESH)
    for c in inputs[:-1]:
        c.wait()

    def copy(src, dst, place, sends, recvs, k):
        return pltpu.make_async_remote_copy(
            src_ref=src,
            dst_ref=dst,
            send_sem=sends.at[k],
            recv_sem=recvs.at[k],
            device_id=place,
            device_id_type=MESH,
        )

    lane1 = iota((1, 128), 1)

    def edges(row):
        last = jnp.where(
            lane1 % GROUP == 0, pltpu.roll(row, 97, 1), pltpu.roll(row, 1, 1)
        )
        return (row * (1 - last) * (lane1 % GROUP)).astype(F32)

    row = aperture_ref[pl.ds(slab, 1), :]
    prev_row = aperture_ref[pl.ds(before, 1), :]
    first_of = edges(row)
    order = iota((16, 64), 0)
    order = jnp.where(order < 8, 2 * (order // 2), 2 * (order // 2) - 7)
    member = iota((16, 64), 1) // 8 == order

    def gates_of(r, half):
        count = jnp.sum(
            jnp.where(lane1 // GROUP == group, r.astype(F32), 0.0), axis=1, keepdims=True
        )
        return jnp.where(
            member & ((order + 8 * half).astype(F32) < count), 1.0 / 32, 0.0
        ).astype(BF16)

    rows_ref[...] = jnp.zeros_like(rows_ref)
    lane8 = iota((8, 128), 1)
    sub8 = iota((8, 128), 0)
    depth = (lane8 & 15).astype(F32)
    side = (lane8 >> 4).astype(F32)
    level = iota((16, 128), 0)
    levels = [(level + 16 * k).astype(BF16) for k in range(4)]
    pasts = [(level + (16 * k - 1)).astype(BF16) for k in range(4)]

    def place_blocks(r):
        source = lax.rem(group + r, 4)
        start = jnp.sum(
            jnp.where(lane1 // GROUP == source, first_of, 0.0), axis=1, keepdims=True
        ).astype(jnp.int32)
        for s in range(2):
            pick = source * GROUP + ((jnp.broadcast_to(start, (8, 128)) + sub8 + 8 * s) & 31)

            def values(ref):
                return jnp.take_along_axis(
                    jnp.broadcast_to(ref[0:1, :], (8, 128)), pick, axis=1
                )

            slope, tilt = values(slope_ref), values(tilt_ref)
            lateral = side + (64 * group).astype(F32)
            place_ref[r, s, 0] = values(offset_ref) + slope * depth + tilt * lateral
            place_ref[r, s, 1] = tilt * 8.0
            place_ref[r, s, 2] = slope * 16.0

    start = run_start(run_ref, 0, group)
    prev_start = run_start(run_ref, 1, group)
    inputs[-1].wait()

    def own_half(half):
        window_sums(
            True, half, start, gates_of(row, half), delay_ref, echo_ref, moved_ref, rows_ref
        )
        own_ref[half] = rows_ref[...]

    own_half(0)
    pl.semaphore_wait(barrier, len(places))
    step = copy(delay_ref, prev_delay_ref, (group, after), ring_send, ring_recv, 0)
    has_before, has_after = slab > 0, slab < SLABS - 1
    pl.when(has_after)(step.start)
    own_half(1)

    @pl.when(jnp.logical_not(has_before))
    def _():
        prev_delay_ref[...] = jnp.zeros_like(prev_delay_ref)

    @pl.when(jnp.logical_not(has_after))
    def _():
        next_ref[...] = jnp.zeros_like(next_ref)

    pl.when(has_before)(step.wait_recv)
    steps = []
    for half in range(2):
        gates = gates_of(prev_row, half)
        window_sums(
            False, half, prev_start, gates, prev_delay_ref, echo_ref, moved_ref, rows_ref
        )
        prev_ref[half] = rows_ref[...].astype(BF16)
        steps.append(
            copy(
                prev_ref.at[half],
                next_ref.at[half],
                (group, before),
                ring_send,
                ring_recv,
                1 + half,
            )
        )
        pl.when(has_before)(steps[half].start)
    for r in range(4):
        place_blocks(r)
    blank = jnp.zeros((128 - ROWS, 128), BF16)
    for t in range(VOXELS // 128):
        beam_ref[t, ROWS:128, :] = blank
        beam_ref[t, 128 + ROWS : 256, :] = blank
    right, left = (lax.rem(group + 1, 4), slab), (lax.rem(group + 3, 4), slab)

    def pass_on(source, target, begin, size, place, k):
        part = pl.ds(begin, size)
        return copy(
            all_ref.at[source, part], all_ref.at[target, part], place, peer_send, peer_recv, k
        )

    near_copies, far_copies = [], []
    for half in range(2):
        begin = half * HALF
        near_copies.append(
            [
                pass_on(0, 3, begin, HALF, right, 4 * half),
                pass_on(0, 1, begin, HALF, left, 4 * half + 1),
            ]
        )
        far_copies.append(
            [
                pass_on(3, 2, begin, HALF // 2, right, 4 * half + 2),
                pass_on(1, 2, begin + HALF // 2, HALF // 2, left, 4 * half + 3),
            ]
        )
    for half in range(2):
        pl.when(has_after)(steps[half].wait_recv)
        all_ref[0, half * HALF : (half + 1) * HALF, :] = (
            own_ref[half] + next_ref[half].astype(F32)
        ).astype(BF16)
        for c in near_copies[half]:
            c.start()

    def weights_of(at, b, skip):
        node, left, right = [
            jnp.broadcast_to(point_ref[at + 8 * k + b : at + 8 * k + b + 1, :], (16, 128)).astype(
                BF16
            )
            for k in range(3)
        ]
        none = jnp.zeros_like(right)
        return jnp.concatenate(
            [
                none
                if k == skip
                else jnp.where(
                    levels[k] == node, left, jnp.where(pasts[k] == node, right, none)
                )
                for k in range(4)
            ],
            axis=0,
        )

    near = 4 - group

    def project(units, first, last):
        lax.fori_loop(0, near, project_tile(units, first, last, 3), 0)
        lax.fori_loop(near, 4, project_tile(units, first, last, 0), 0)

    def project_tile(units, first, last, skip):
        def tile(i, carry):
            at = 0
            for v in range(4):
                for r, s in units:
                    base = place_ref[r, s, 0] + place_ref[r, s, 2] * i.astype(F32)
                    for u in range(2):
                        position = base + place_ref[r, s, 1] * float(2 * v + u)
                        node = jnp.floor(position)
                        right = position - node
                        point_ref[at : at + 8, :] = node
                        point_ref[at + 8 : at + 16, :] = 1.0 - right
                        point_ref[at + 16 : at + 24, :] = right
                        at += 24
            at = 0
            for v in range(4):
                n = 4 * i + v
                columns = pl.ds(pl.multiple_of(n * 256, 256), 256)
                total = None if first else total_ref[:, columns]
                for r, s in units:
                    for c in range(2):
                        weights = jnp.concatenate(
                            [
                                jnp.concatenate(
                                    [weights_of(at, b, skip), weights_of(at + 24, b, skip)],
                                    axis=1,
                                )
                                for b in range(4 * c, 4 * c + 4)
                            ],
                            axis=0,
                        )
                        m = 4 * s + 2 * c
                        blocks = jnp.concatenate(
                            [
                                all_ref[r, m * ROWS : (m + 1) * ROWS, :],
                                all_ref[r, (m + 1) * ROWS : (m + 2) * ROWS, :],
                            ],
                            axis=1,
                        )
                        part = jnp.dot(blocks, weights, preferred_element_type=F32)
                        total = part if total is None else total + part
                    at += 48
                if not last:
                    total_ref[:, columns] = total
                    continue
                high = total.astype(BF16)
                low = (total - high.astype(F32)).astype(BF16)
                for q in range(2):
                    lanes = slice(q * 128, q * 128 + 128)
                    beam_ref[2 * n + q, 0:ROWS, :] = high[:, lanes]
                    beam_ref[2 * n + q, 128 : 128 + ROWS, :] = low[:, lanes]
            return carry

        return tile

    project(((0, 0), (0, 1)), True, False)
    for half in range(2):
        for k in range(2):
            near_copies[half][k].wait_recv()
            far_copies[half][k].start()
        project(((3, half), (1, half)), False, False)
    for c in far_copies[0] + far_copies[1]:
        c.wait_recv()
    project(((2, 0), (2, 1)), False, True)
    pl.when(has_after)(step.wait_send)
    for half in range(2):
        pl.when(has_before)(steps[half].wait_send)
        for c in near_copies[half] + far_copies[half]:
            c.wait_send()
    wide_ref[...] = jnp.zeros_like(wide_ref)

    def square(i, carry):
        part = jnp.concatenate([beam_ref[8 * i + k] for k in range(8)], axis=1)
        wide_ref[...] += lax.dot_general(
            part, part[0:128], (((1,), (1,)), ((), ())), preferred_element_type=F32
        )
        return carry

    lax.fori_loop(0, 4, square, 0)
    cross = wide_ref[128:256, :]
    gram = wide_ref[0:128, :] + cross + cross.T
    for k in range(32):
        mine_ref[k] = gram[4 * k : 4 * k + 4]

    def exchange(copies):
        for c in copies:
            c.start()
        for c in copies:
            c.wait()

    exchange(
        [
            copy(mine_ref.at[peer], got_ref.at[k], place, send, recv, k)
            for k, (peer, place) in enumerate(around)
        ]
    )
    total = mine_ref[me]
    for k in range(31):
        total = total + got_ref[k]
    sum_ref[...] = total
    exchange(
        [
            copy(sum_ref, got_ref.at[31 + k], place, send, recv, 31 + k)
            for k, place in enumerate(along_z)
        ]
    )
    for k in range(7):
        total = total + got_ref[31 + k]
    gram_ref[me] = total
    exchange(
        [
            copy(gram_ref.at[me], gram_ref.at[me], place, send, recv, 38 + k)
            for k, (_, place) in enumerate(around)
        ]
    )

    gram = jnp.concatenate([gram_ref[k] for k in range(32)], axis=0)
    basis_ref[...] = jnp.zeros_like(basis_ref)
    basis_ref[0:RANK, 0:FRAMES] = prior_ref[...]
    lane = iota((32, 128), 1)
    odd = (lane >= SIDE).astype(jnp.int32)
    frame = 2 * (lane - SIDE * odd) + odd
    basis = jnp.take_along_axis(basis_ref[...], jnp.minimum(frame, 127), axis=1)
    basis = jnp.where(frame < FRAMES, basis, 0.0)
    basis = sweep(gram, basis)
    basis = sweep(gram, basis)
    overlap = lax.dot_general(
        basis,
        basis,
        (((0,), (0,)), ((), ())),
        precision=lax.Precision.HIGHEST,
        preferred_element_type=F32,
    )
    keep = jnp.where(iota((128, 128), 0) == iota((128, 128), 1), 1.0, 0.0) - overlap
    high = keep.astype(BF16)
    low = (keep - high.astype(F32)).astype(BF16)
    twice = jnp.concatenate([high, high], axis=1)
    for c in range(VOXELS // 256):
        beam = jnp.concatenate([beam_ref[2 * c], beam_ref[2 * c + 1]], axis=1)
        clean = jnp.dot(twice, beam, preferred_element_type=F32)
        clean = clean + jnp.dot(low, beam[0:128], preferred_element_type=F32)
        power = jnp.sum(clean * clean, axis=0, keepdims=True)
        power_ref[2 * c : 2 * c + 1, :] = power[:, 0:128]
        power_ref[2 * c + 1 : 2 * c + 2, :] = power[:, 128:256]
    pick = (2 * (sub8 & 3) + (lane8 >> 6)) * 16 + (lane8 & 15)
    quarter = (lane8 >> 4) & 3
    for p in range(4):
        rows = None
        for q in range(4):
            one = jnp.broadcast_to(power_ref[8 * q + 2 * p : 8 * q + 2 * p + 1, :], (8, 128))
            two = jnp.broadcast_to(power_ref[8 * q + 2 * p + 1 : 8 * q + 2 * p + 2, :], (8, 128))
            got = jnp.take_along_axis(jnp.where(sub8 < 4, one, two), pick, axis=1)
            rows = got if rows is None else jnp.where(quarter == q, got, rows)
        out_ref[8 * p : 8 * p + 8, :] = rows


def body(echo_data, delays, aperture, offset, depth_slope, lateral_tilt, prior_basis):
    vmem = pl.BlockSpec(memory_space=VMEM)
    dma = pltpu.SemaphoreType.DMA
    squares = pl.pallas_call(
        kernel,
        out_shape=VMEM((VOXELS // 128, 128), F32),
        in_specs=[pl.BlockSpec(memory_space=pl.ANY)] * 7,
        out_specs=vmem,
        scratch_shapes=[
            pltpu.SMEM((2, 128), jnp.int32),
            VMEM((SLABS, 128), jnp.int32),
            VMEM((1, 256), jnp.int32),
            VMEM((1, 128), F32),
            VMEM((1, 128), F32),
            VMEM((1, 128), F32),
            VMEM((RANK, FRAMES), F32),
            VMEM((GROUP, 8, 128 * PAIRS), BF16),
            VMEM((PAIRS, 64, 128), BF16),
            VMEM((HALF, 128), F32),
            VMEM((2, HALF, 128), F32),
            VMEM((2, HALF, 128), BF16),
            VMEM((2, HALF, 128), BF16),
            VMEM((1, 256), jnp.int32),
            VMEM((4, SIZE, 128), BF16),
            VMEM((4, 2, 3, 8, 128), F32),
            VMEM((384, 128), F32),
            VMEM((ROWS, VOXELS), F32),
            VMEM((VOXELS // 128, 256, 128), BF16),
            VMEM((256, 128), F32),
            VMEM((32, 4, 128), F32),
            VMEM((38, 4, 128), F32),
            VMEM((4, 128), F32),
            VMEM((32, 4, 128), F32),
            VMEM((32, 128), F32),
            VMEM((VOXELS // 128, 128), F32),
            dma((9,)),
            dma((3,)),
            dma((3,)),
            dma((8,)),
            dma((8,)),
            dma((69,)),
            dma((69,)),
        ],
        compiler_params=pltpu.CompilerParams(
            collective_id=0, has_side_effects=True, vmem_limit_bytes=62 * 1024 * 1024
        ),
        name="doppler",
    )(
        aperture.T,
        delays.reshape(1, 256),
        offset.reshape(1, 128),
        depth_slope.reshape(1, 128),
        lateral_tilt.reshape(1, 128),
        prior_basis.T,
        echo_data.reshape(GROUP, 8, 128 * PAIRS),
    )
    return squares.reshape(1, VOXELS) / FRAMES


def solution(mesh):
    in_specs = (
        P("chan", "vox", None),
        P("chan", "vox"),
        P(),
        P(None, "vox"),
        P(None, "vox"),
        P(None, "vox"),
        P(),
    )
    out_specs = P("vox", "chan")
    return jax.shard_map(body, mesh=mesh, in_specs=in_specs, out_specs=out_specs, check_vma=False)
```

time: 57 us -> 49.7 us (0.87)
  Pallas kernels: 55.4 us -> 49 us
  other arithmetic: 1.34 us -> 0.61 us
    pallas_call x1, Pallas kernels: 55.4 us -> 49 us  [body(): pl.pallas_call(kernel, out_shape=VMEM((VOXELS // 128, 128), F32), in_spec...]
    div x1, other arithmetic: 1.34 us -> 0.61 us  [body(): return squares.reshape(1, VOXELS) / FRAMES]
where the time goes in v4:
time: 49.7 us; the launch traced here: 49.6 us
  Pallas kernels  49 us (99%)
  other arithmetic  0.61 us (1%)
    pallas_call x1, Pallas kernels, body(): pl.pallas_call(kernel, out_shape=VMEM((VOXELS // 128, 128), F32), in_spec...  49 us

profile of v4, /device:TPU:1, one launch (start us, length us, event | category | flops | bytes accessed | tf_op | source)
XLA Modules:
  0.0 49.6 jit_solution(12732172200394539976)
XLA Ops:
  0.0 49.0 %doppler.1 = f32[32,128]{1,0:T(8,128)S(1)} custom-call(s32[64,128]{1,0:T(8,128)} %bitcast.9, s32[1,256]{1,0:T(1,128)} %bitcast.11, f32[1,128]{1,0:T(1,128)} %bitcast.12, f32[1,128]{1,0:T(1,128)} %bitcast.13, f32[1,128]{1,0:T(1,128)} %bitcast.14, f32[30,100]{1,0:T(8,128)} %bitcast.10, bf16[32,8,6400]{2,1,0:T(8,128)(2,1)} %bitcast.8), custom_call_target="tpu_custom_call" | custom-call | tf_op jit(solution)/shard_map/doppler/pallas_call | solution.py:530
  49.0 0.6 %broadcast_multiply_fusion = f32[32,128]{1,0:T(8,128)} fusion(f32[32,128]{1,0:T(8,128)S(1)} %doppler.1), kind=kLoop, calls=%fused_computation | loop fusion | flops 4096 | bytes 32768 | tf_op jit(solution)/shard_map/div | solution.py:583

commit v5 on v4

--- a/solution.py
+++ b/solution.py
@@ -165,16 +165,16 @@
     y, z = chip // 8, lax.rem(chip, 8)
     me = y * 8 + group * 2 + core
     around = []
-    for dy in range(4):
+    for dy in (2, 1, 3, 0):
         row_y = lax.rem(y + dy, 4)
-        for d in range(8):
+        for d in (4, 3, 5, 2, 6, 1, 7, 0):
             if dy == 0 and d == 0:
                 continue
             inner = lax.rem(group * 2 + core + d, 8)
             around.append(
                 (row_y * 8 + inner, (inner // 2, (row_y * 8 + z) * 2 + lax.rem(inner, 2)))
             )
-    along_z = [(group, (y * 8 + lax.rem(z + d, 8)) * 2 + core) for d in range(1, 8)]
+    along_z = [(group, (y * 8 + lax.rem(z + d, 8)) * 2 + core) for d in (4, 3, 5, 2, 6, 1, 7)]
     inputs = [
         pltpu.make_async_copy(source, target, input_sem.at[k])
         for k, (source, target) in enumerate(
@@ -194,7 +194,7 @@
     for c in inputs:
         c.start()
     barrier = pltpu.get_barrier_semaphore()
-    places = along_z + [a[1] for a in around[::-1]] + [(group, before), (group, after)]
+    places = along_z + [a[1] for a in around] + [(group, before), (group, after)]
     for place in places:
         pl.semaphore_signal(barrier, inc=1, device_id=place, device_id_type=MESH)
     for c in inputs[:-1]:
@@ -452,36 +452,37 @@
     for k in range(32):
         mine_ref[k] = gram[4 * k : 4 * k + 4]
 
-    def exchange(copies):
-        for c in copies:
-            c.start()
-        for c in copies:
-            c.wait()
+    def exchange(stage, moves, all_sent, all_received):
+        for source, target, place in moves:
+            copy(source, target, place, send, recv, stage).start()
+        every = copy(all_sent, all_received, moves[0][2], send, recv, stage)
+        every.wait_recv()
+        every.wait_send()
 
     exchange(
-        [
-            copy(mine_ref.at[peer], got_ref.at[k], place, send, recv, k)
-            for k, (peer, place) in enumerate(around)
-        ]
+        0,
+        [(mine_ref.at[peer], got_ref.at[k], place) for k, (peer, place) in enumerate(around)],
+        mine_ref.at[0:31],
+        got_ref.at[0:31],
     )
     total = mine_ref[me]
     for k in range(31):
         total = total + got_ref[k]
     sum_ref[...] = total
     exchange(
-        [
-            copy(sum_ref, got_ref.at[31 + k], place, send, recv, 31 + k)
-            for k, place in enumerate(along_z)
-        ]
+        1,
+        [(sum_ref, got_ref.at[31 + k], place) for k, place in enumerate(along_z)],
+        mine_ref.at[0:7],
+        got_ref.at[31:38],
     )
     for k in range(7):
         total = total + got_ref[31 + k]
     gram_ref[me] = total
     exchange(
-        [
-            copy(gram_ref.at[me], gram_ref.at[me], place, send, recv, 38 + k)
-            for k, (_, place) in enumerate(around)
-        ]
+        2,
+        [(gram_ref.at[me], gram_ref.at[me], place) for _, place in around],
+        mine_ref.at[0:31],
+        gram_ref.at[0:31],
     )
 
     gram = jnp.concatenate([gram_ref[k] for k in range(32)], axis=0)
@@ -564,8 +565,8 @@
             dma((3,)),
             dma((8,)),
             dma((8,)),
-            dma((69,)),
-            dma((69,)),
+            dma((3,)),
+            dma((3,)),
         ],
         compiler_params=pltpu.CompilerParams(
             collective_id=0, has_side_effects=True, vmem_limit_bytes=62 * 1024 * 1024

time: 49.7 us -> 48 us (0.966)
  Pallas kernels: 49 us -> 47.3 us
    pallas_call x1, Pallas kernels: 49 us -> 47.3 us  [body(): pl.pallas_call(kernel, out_shape=VMEM((VOXELS // 128, 128), F32), in_spec...]
where the time goes in v5:
time: 48 us; the launch traced here: 47.9 us
  Pallas kernels  47.3 us (99%)
  other arithmetic  0.61 us (1%)
    pallas_call x1, Pallas kernels, body(): pl.pallas_call(kernel, out_shape=VMEM((VOXELS // 128, 128), F32), in_spec...  47.3 us

profile of v5, /device:TPU:1, one launch (start us, length us, event | category | flops | bytes accessed | tf_op | source)
XLA Modules:
  0.0 47.9 jit_solution(13022958053889993135)
XLA Ops:
  0.0 47.3 %doppler.1 = f32[32,128]{1,0:T(8,128)S(1)} custom-call(s32[64,128]{1,0:T(8,128)} %bitcast.9, s32[1,256]{1,0:T(1,128)} %bitcast.11, f32[1,128]{1,0:T(1,128)} %bitcast.12, f32[1,128]{1,0:T(1,128)} %bitcast.13, f32[1,128]{1,0:T(1,128)} %bitcast.14, f32[30,100]{1,0:T(8,128)} %bitcast.10, bf16[32,8,6400]{2,1,0:T(8,128)(2,1)} %bitcast.8), custom_call_target="tpu_custom_call" | custom-call | tf_op jit(solution)/shard_map/doppler/pallas_call | solution.py:531
  47.3 0.6 %broadcast_multiply_fusion = f32[32,128]{1,0:T(8,128)} fusion(f32[32,128]{1,0:T(8,128)S(1)} %doppler.1), kind=kLoop, calls=%fused_computation | loop fusion | flops 4096 | bytes 32768 | tf_op jit(solution)/shard_map/div | solution.py:584

commit v6 on v5

--- a/solution.py
+++ b/solution.py
@@ -148,6 +148,7 @@
     gram_ref,
     basis_ref,
     power_ref,
+    ready_sem,
     input_sem,
     ring_send,
     ring_recv,
@@ -194,7 +195,9 @@
     for c in inputs:
         c.start()
     barrier = pltpu.get_barrier_semaphore()
-    places = along_z + [a[1] for a in around] + [(group, before), (group, after)]
+    along_y = [(group, (lax.rem(y + d, 4) * 8 + z) * 2 + core) for d in (2, 1, 3)]
+    beside = [place for k, (_, place) in enumerate(around) if k >= 24]
+    places = beside + along_y + [(group, before), (group, after)] + along_z
     for place in places:
         pl.semaphore_signal(barrier, inc=1, device_id=place, device_id_type=MESH)
     for c in inputs[:-1]:
@@ -263,19 +266,21 @@
 
     start = run_start(run_ref, 0, group)
     prev_start = run_start(run_ref, 1, group)
-    inputs[-1].wait()
 
     def own_half(half):
         window_sums(
             True, half, start, gates_of(row, half), delay_ref, echo_ref, moved_ref, rows_ref
         )
-        own_ref[half] = rows_ref[...]
-
-    own_half(0)
+        own_ref[half] = rows_ref[0:HALF, :]
+
     pl.semaphore_wait(barrier, len(places))
     step = copy(delay_ref, prev_delay_ref, (group, after), ring_send, ring_recv, 0)
     has_before, has_after = slab > 0, slab < SLABS - 1
     pl.when(has_after)(step.start)
+    for place in along_y:
+        pl.semaphore_signal(ready_sem, inc=1, device_id=place, device_id_type=MESH)
+    inputs[-1].wait()
+    own_half(0)
     own_half(1)
 
     @pl.when(jnp.logical_not(has_before))
@@ -293,7 +298,7 @@
         window_sums(
             False, half, prev_start, gates, prev_delay_ref, echo_ref, moved_ref, rows_ref
         )
-        prev_ref[half] = rows_ref[...].astype(BF16)
+        prev_ref[half] = rows_ref[0:HALF, :].astype(BF16)
         steps.append(
             copy(
                 prev_ref.at[half],
@@ -440,13 +445,13 @@
     wide_ref[...] = jnp.zeros_like(wide_ref)
 
     def square(i, carry):
-        part = jnp.concatenate([beam_ref[8 * i + k] for k in range(8)], axis=1)
+        part = jnp.concatenate([beam_ref[16 * i + k] for k in range(16)], axis=1)
         wide_ref[...] += lax.dot_general(
             part, part[0:128], (((1,), (1,)), ((), ())), preferred_element_type=F32
         )
         return carry
 
-    lax.fori_loop(0, 4, square, 0)
+    lax.fori_loop(0, 2, square, 0)
     cross = wide_ref[128:256, :]
     gram = wide_ref[0:128, :] + cross + cross.T
     for k in range(32):
@@ -459,6 +464,7 @@
         every.wait_recv()
         every.wait_send()
 
+    pl.semaphore_wait(ready_sem, 3)
     exchange(
         0,
         [(mine_ref.at[peer], got_ref.at[k], place) for k, (peer, place) in enumerate(around)],
@@ -543,7 +549,7 @@
             VMEM((RANK, FRAMES), F32),
             VMEM((GROUP, 8, 128 * PAIRS), BF16),
             VMEM((PAIRS, 64, 128), BF16),
-            VMEM((HALF, 128), F32),
+            VMEM((HALF + 56, 128), F32),
             VMEM((2, HALF, 128), F32),
             VMEM((2, HALF, 128), BF16),
             VMEM((2, HALF, 128), BF16),
@@ -560,6 +566,7 @@
             VMEM((32, 4, 128), F32),
             VMEM((32, 128), F32),
             VMEM((VOXELS // 128, 128), F32),
+            pltpu.SemaphoreType.REGULAR,
             dma((9,)),
             dma((3,)),
             dma((3,)),

time: 48 us -> 46.3 us (0.965)
  Pallas kernels: 47.3 us -> 45.6 us
    pallas_call x1, Pallas kernels: 47.3 us -> 45.6 us  [body(): pl.pallas_call(kernel, out_shape=VMEM((VOXELS // 128, 128), F32), in_spec...]
where the time goes in v6:
time: 46.3 us; the launch traced here: 46.2 us
  Pallas kernels  45.6 us (98%)
  other arithmetic  0.61 us (1%)
    pallas_call x1, Pallas kernels, body(): pl.pallas_call(kernel, out_shape=VMEM((VOXELS // 128, 128), F32), in_spec...  45.6 us

profile of v6, /device:TPU:1, one launch (start us, length us, event | category | flops | bytes accessed | tf_op | source)
XLA Modules:
  0.0 46.2 jit_solution(7147899118742496991)
XLA Ops:
  0.0 45.6 %doppler.1 = f32[32,128]{1,0:T(8,128)S(1)} custom-call(s32[64,128]{1,0:T(8,128)} %bitcast.9, s32[1,256]{1,0:T(1,128)} %bitcast.11, f32[1,128]{1,0:T(1,128)} %bitcast.12, f32[1,128]{1,0:T(1,128)} %bitcast.13, f32[1,128]{1,0:T(1,128)} %bitcast.14, f32[30,100]{1,0:T(8,128)} %bitcast.10, bf16[32,8,6400]{2,1,0:T(8,128)(2,1)} %bitcast.8), custom_call_target="tpu_custom_call" | custom-call | tf_op jit(solution)/shard_map/doppler/pallas_call | solution.py:537
  45.6 0.6 %broadcast_multiply_fusion = f32[32,128]{1,0:T(8,128)} fusion(f32[32,128]{1,0:T(8,128)S(1)} %doppler.1), kind=kLoop, calls=%fused_computation | loop fusion | flops 4096 | bytes 32768 | tf_op jit(solution)/shard_map/div | solution.py:591

commit v7 on v6

--- a/solution.py
+++ b/solution.py
@@ -462,29 +462,35 @@
             copy(source, target, place, send, recv, stage).start()
         every = copy(all_sent, all_received, moves[0][2], send, recv, stage)
         every.wait_recv()
-        every.wait_send()
+        return every
+
+    def added(values):
+        while len(values) > 1:
+            values = [
+                values[i] + values[i + 1] if i + 1 < len(values) else values[i]
+                for i in range(0, len(values), 2)
+            ]
+        return values[0]
 
     pl.semaphore_wait(ready_sem, 3)
-    exchange(
+    stages = [None] * 3
+    stages[0] = exchange(
         0,
         [(mine_ref.at[peer], got_ref.at[k], place) for k, (peer, place) in enumerate(around)],
         mine_ref.at[0:31],
         got_ref.at[0:31],
     )
-    total = mine_ref[me]
-    for k in range(31):
-        total = total + got_ref[k]
+    total = added([mine_ref[me]] + [got_ref[k] for k in range(31)])
     sum_ref[...] = total
-    exchange(
+    stages[1] = exchange(
         1,
         [(sum_ref, got_ref.at[31 + k], place) for k, place in enumerate(along_z)],
         mine_ref.at[0:7],
         got_ref.at[31:38],
     )
-    for k in range(7):
-        total = total + got_ref[31 + k]
+    total = added([total] + [got_ref[31 + k] for k in range(7)])
     gram_ref[me] = total
-    exchange(
+    stages[2] = exchange(
         2,
         [(gram_ref.at[me], gram_ref.at[me], place) for _, place in around],
         mine_ref.at[0:31],
@@ -519,6 +525,8 @@
         power = jnp.sum(clean * clean, axis=0, keepdims=True)
         power_ref[2 * c : 2 * c + 1, :] = power[:, 0:128]
         power_ref[2 * c + 1 : 2 * c + 2, :] = power[:, 128:256]
+    for stage in stages:
+        stage.wait_send()
     pick = (2 * (sub8 & 3) + (lane8 >> 6)) * 16 + (lane8 & 15)
     quarter = (lane8 >> 4) & 3
     for p in range(4):

time: 46.3 us -> 46.3 us (level)
  no operation moved by 1% of the time
where the time goes in v7:
time: 46.3 us; the launch traced here: 46.2 us
  Pallas kernels  45.6 us (98%)
  other arithmetic  0.61 us (1%)
    pallas_call x1, Pallas kernels, body(): pl.pallas_call(kernel, out_shape=VMEM((VOXELS // 128, 128), F32), in_spec...  45.6 us

profile of v7, /device:TPU:1, one launch (start us, length us, event | category | flops | bytes accessed | tf_op | source)
XLA Modules:
  0.0 46.2 jit_solution(5097375050285152779)
XLA Ops:
  0.0 45.6 %doppler.1 = f32[32,128]{1,0:T(8,128)S(1)} custom-call(s32[64,128]{1,0:T(8,128)} %bitcast.9, s32[1,256]{1,0:T(1,128)} %bitcast.11, f32[1,128]{1,0:T(1,128)} %bitcast.12, f32[1,128]{1,0:T(1,128)} %bitcast.13, f32[1,128]{1,0:T(1,128)} %bitcast.14, f32[30,100]{1,0:T(8,128)} %bitcast.10, bf16[32,8,6400]{2,1,0:T(8,128)(2,1)} %bitcast.8), custom_call_target="tpu_custom_call" | custom-call | tf_op jit(solution)/shard_map/doppler/pallas_call | solution.py:545
  45.6 0.6 %broadcast_multiply_fusion = f32[32,128]{1,0:T(8,128)} fusion(f32[32,128]{1,0:T(8,128)S(1)} %doppler.1), kind=kLoop, calls=%fused_computation | loop fusion | flops 4096 | bytes 32768 | tf_op jit(solution)/shard_map/div | solution.py:599
